TPU v7x, 512 devices: a whole 4x4x16 slice. The times are simulated.
512 devices in a mesh: seq: 64 (over z, y), exp: 8 (over x, core).
Axes of the slice: x: 4, y: 4, z: 16, core: 2. Of those that a mesh axis runs over, the one named last changes fastest.
Arguments:
- x_in: bfloat16 [4096, 8192], P('seq', 'exp'), may hold values from -6 to 6
- z_gate: bfloat16 [4096, 8192], P('seq', 'exp'), may hold values from -6 to 6
- dt_low: bfloat16 [4096, 256], P('seq'), may hold values from -6 to 6
- dt_weight: bfloat16 [256, 8192], P(None, 'exp'), may hold values from -0.375 to 0.375
- dt_bias: float32 [8192], P('exp'), may hold values from -9 to -1
- a_log: float32 [16, 8192], P(None, 'exp'), may hold values from -4 to 0
- conv_weight: float32 [4, 8192], P(None, 'exp'), may hold values from -3 to 3
- conv_bias: float32 [8192], P('exp'), may hold values from -0.5 to 0.5
- d_skip: float32 [8192], P('exp'), may hold values from 0.5 to 1.5
- b_and_c: float32 [2, 16, 4096], P(None, None, 'seq'), may hold values from -6 to 6
- hidden: bfloat16 [4096, 4096], P('seq', 'exp'), may hold values from -6 to 6
- router: bfloat16 [4096, 8], P('exp'), may hold values from -0.09375 to 0.09375
- expert_ids: int32 [4096, 2], P('seq'), may hold values from 0 to 7, all different within a row; in each aligned block of 64 rows (0 to 63, 64 to 127, ...) at most 18 rows name the same one
- w_gate: bfloat16 [4096, 98304], P('exp', 'seq'), may hold values from -0.09375 to 0.09375
- w_down: bfloat16 [98304, 4096], P('seq', 'exp'), may hold values from -0.0546875 to 0.0546875
Outputs:
- mamba_out: bfloat16 [4096, 8192], P('seq', 'exp')
- moe_out: bfloat16 [4096, 4096], P('seq', 'exp')
Inputs may be any that keep to these rules, and one draw needn't show every extreme that they name: `expert_ids`: each token names 2 different experts; among the 64 tokens of one block no expert is named more than 18 times, a bound that some expert reaches in every block.
All inputs are finite; a program needn't handle non-finite values.
Results may differ from a plain program's by a relative error of at most 0.018.
Values may be sent and summed in bfloat16 or wider, within the bound.
A program may use at most 128 MiB of HBM per device.

v0:
```python
import jax
import jax.numpy as jnp
from jax import lax
from jax.sharding import PartitionSpec as P

CAP = 18


def passed_along(value, axis, steps):
    count = lax.axis_size(axis)
    first, last = (max(0, -steps), min(count, count - steps))
    return lax.ppermute(value, axis, [(source, source + steps) for source in range(first, last)])


def carried_in(array, axis, join, neutral):
    place = lax.axis_index(axis)
    gathered = jax.tree.map(
        lambda a, kind: lax.all_gather(a.astype(kind), axis), array, (jnp.bfloat16, jnp.bfloat16)
    )
    state = jax.tree.map(lambda a, e: jnp.zeros_like(a) + jnp.asarray(e, a.dtype), array, neutral)

    def one(lap, state):
        return join(
            state,
            jax.tree.map(
                lambda a, own: lax.dynamic_index_in_dim(a, lap, 0, False).astype(own.dtype),
                gathered,
                array,
            ),
        )

    return lax.fori_loop(0, place, one, state)


def link_pairs(earlier, later):
    return (earlier[0] * later[0], later[0] * earlier[1] + later[1])


def mixer_scan(delta, activated, b_rows, c_rows, rates, start_state):
    token_count, channels = delta.shape
    block_len = 16
    block_count = token_count // block_len

    def regroup(values):
        return values.reshape((block_count, block_len) + values.shape[1:])

    def advance(carry, inputs):
        running, product = carry
        step_delta, step_x, step_b, step_c = inputs
        reads = []
        for position in range(block_len):
            factor = jnp.exp(step_delta[position][None, :] * rates)
            running = (
                factor * running
                + step_b[position][:, None] * (step_delta[position] * step_x[position])[None, :]
            )
            product = factor * product
            reads.append(jnp.sum(step_c[position][:, None] * running, axis=0))
        return ((running, product), (jnp.stack(reads),))

    initial = (start_state, jnp.ones(rates.shape, jnp.float32))
    finals, outputs = lax.scan(
        advance, initial, (regroup(delta), regroup(activated), regroup(b_rows), regroup(c_rows))
    )
    readout = outputs[0].reshape(token_count, channels)
    weighted_all = None
    return (readout, weighted_all, finals[0], finals[1])


def local(
    x_in,
    z_gate,
    dt_low,
    dt_weight,
    dt_bias,
    a_log,
    conv_weight,
    conv_bias,
    d_skip,
    b_and_c,
    hidden,
    router,
    expert_ids,
    w_gate,
    w_down,
):
    tok_rows = x_in.shape[0]
    kernel_taps = conv_weight.shape[0]
    edge_rows = passed_along(x_in[tok_rows - (kernel_taps - 1) :], "seq", 1)
    padded = jnp.concatenate([edge_rows, x_in], axis=0).astype(jnp.float32)
    convolved = jnp.zeros(x_in.shape, jnp.float32) + conv_bias[None, :]
    for offset in range(kernel_taps):
        convolved = convolved + conv_weight[offset][None, :] * padded[offset : offset + tok_rows]
    activated = jax.nn.silu(convolved)
    delta = jax.nn.softplus(
        jnp.dot(dt_low, dt_weight, preferred_element_type=jnp.float32) + dt_bias[None, :]
    )
    rates = -jnp.exp(a_log)
    b_rows = b_and_c[0].T
    c_rows = b_and_c[1].T
    zero_state = jnp.zeros(rates.shape, jnp.float32)
    readout, weighted_all, end_state, end_product = mixer_scan(
        delta, activated, b_rows, c_rows, rates, zero_state
    )
    identity = (jnp.ones(rates.shape, jnp.float32), jnp.zeros(rates.shape, jnp.float32))
    carried = carried_in((end_product, end_state), "seq", link_pairs, identity)
    entering = carried[1]
    readout = mixer_scan(delta, activated, b_rows, c_rows, rates, entering)[0]
    mamba_out = (
        (readout + d_skip[None, :] * activated) * jax.nn.silu(z_gate.astype(jnp.float32))
    ).astype(jnp.bfloat16)
    experts = router.shape[1]
    picks = expert_ids.shape[1]
    feature_width = hidden.shape[1]
    group_size = lax.axis_size("seq") // experts
    logits = lax.psum(jnp.dot(hidden, router, preferred_element_type=jnp.float32), "exp")
    expert_iota = lax.broadcasted_iota(jnp.int32, (1, 1, experts), 2)
    chosen = expert_ids[:, :, None] == expert_iota
    picked = jnp.sum(jnp.where(chosen, logits[:, None, :], 0.0), axis=2)
    gates = jax.nn.sigmoid(picked - picked[:, ::-1])
    flat_hits = chosen.reshape(tok_rows * picks, experts).astype(jnp.int32)
    earlier_hits = jnp.cumsum(flat_hits, axis=0) - flat_hits
    slots = jnp.sum(earlier_hits * flat_hits, axis=1).reshape(tok_rows, picks)
    slot_keys = expert_ids * CAP + slots
    slot_iota = lax.broadcasted_iota(jnp.int32, (experts * CAP, 1, 1), 0)
    matches = slot_keys[None] == slot_iota
    selector = jnp.sum(matches.astype(jnp.float32), axis=2).astype(jnp.bfloat16)
    blending = jnp.sum(jnp.where(matches, gates[None], 0.0), axis=2)
    packed = jnp.dot(selector, hidden, preferred_element_type=jnp.float32).astype(jnp.bfloat16)
    outgoing = jnp.broadcast_to(
        packed.reshape(experts, 1, CAP, feature_width), (experts, group_size, CAP, feature_width)
    )
    outgoing = outgoing.reshape(experts * group_size, CAP, feature_width)
    arrived = lax.all_to_all(outgoing, "seq", split_axis=0, concat_axis=0, tiled=True)
    sources, entries, features = arrived.shape
    routed = arrived.reshape(sources * entries, features)
    partial_value = jnp.dot(routed, w_gate, preferred_element_type=jnp.float32)
    summed = lax.psum(partial_value.astype(jnp.bfloat16), "exp").astype(jnp.float32)
    acted = jax.nn.silu(summed).astype(jnp.bfloat16)
    produced = jnp.dot(acted, w_down, preferred_element_type=jnp.float32)
    produced = produced.reshape(sources, entries, features)
    returned = lax.all_to_all(
        produced.astype(jnp.bfloat16), "seq", split_axis=0, concat_axis=0, tiled=True
    ).astype(produced.dtype)
    combined = jnp.sum(returned.reshape(experts, group_size, CAP, feature_width), axis=1).reshape(
        experts * CAP, feature_width
    )
    moe_out = jnp.einsum("rt,rd->td", blending, combined, precision=lax.Precision.HIGHEST)
    return (mamba_out, moe_out.astype(jnp.bfloat16))


def solution(mesh):
    return jax.shard_map(
        local,
        mesh=mesh,
        in_specs=(
            P("seq", "exp"),
            P("seq", "exp"),
            P("seq", None),
            P(None, "exp"),
            P("exp"),
            P(None, "exp"),
            P(None, "exp"),
            P("exp"),
            P("exp"),
            P(None, None, "seq"),
            P("seq", "exp"),
            P("exp", None),
            P("seq", None),
            P("exp", "seq"),
            P("seq", "exp"),
        ),
        out_specs=(P("seq", "exp"), P("seq", "exp")),
        check_vma=False,
    )
```

profile of v0, /device:TPU:6, one launch (start us, length us, event | category | flops | bytes accessed | tf_op | source)
XLA Modules:
  0.0 475.2 jit_solution(18132872191936348174)
XLA Ops:
  8.1 0.8 slice.515
  8.9 3.5 collective-permute-start
  12.4 0.9 fusion.108
  13.3 0.9 exponential_negate_fusion
  14.1 1.4 compare_select_fusion
  15.5 1.3 slice_bitcast_fusion
  16.9 0.9 maximum_convert_fusion
  17.8 0.9 divide_multiply_fusion
  18.7 4.2 while.39
  18.8 0.2 constant_dynamic-slice_fusion.115
  19.3 0.3 multiply_add_fusion.23
  19.6 0.2 fusion.126
  19.9 0.2 constant_dynamic-slice_fusion.115
  20.3 0.3 multiply_add_fusion.23
  20.7 0.2 fusion.126
  20.9 0.2 constant_dynamic-slice_fusion.115
  21.4 0.3 multiply_add_fusion.23
  21.7 0.2 fusion.126
  22.0 0.2 constant_dynamic-slice_fusion.115
  22.4 0.3 multiply_add_fusion.23
  22.7 0.2 fusion.126
  22.9 0.7 convert_element_type.61
  23.9 12.1 %psum.14 = f32[64,8]{0,1:T(8,128)S(1)} all-reduce(f32[64,8]{0,1:T(8,128)S(1)} %fusion.109), channel_id=1, replica_groups=mesh['seq'=64,'exp'=8] {'exp'}, use_global_device_ids=true, to_apply=%region_24.25 | all-reduce | flops 512 | bytes 4096 | tf_op jit(solution)/shard_map/psum | solution.py:116
  36.3 0.2 reduce_window_sum.11
  36.5 0.2 select_reduce_fusion.1
  36.6 0.1 reshape.655
  36.9 0.7 convert_reduce_fusion.1
  37.6 0.2 convolution_convert_fusion.1
  37.9 1.3 broadcast_in_dim.47
  39.1 16.5 %all-to-all-start = ((bf16[64,18,512]{2,1,0:T(8,128)(2,1)}), bf16[64,18,512]{2,1,0:T(8,128)(2,1)S(1)}, u32[]{:S(2)}, u32[]{:S(2)}) async-start(bf16[64,18,512]{2,1,0:T(8,128)(2,1)} %bitcast.98), calls=%async_computation | async-start | bytes 3145728 | tf_op jit(solution)/shard_map/all_to_all | solution.py:134
  55.7 1.4 convert_element_type.62
  57.2 76.9 %all-to-all-done = bf16[64,18,512]{2,1,0:T(8,128)(2,1)S(1)} async-done(((bf16[64,18,512]{2,1,0:T(8,128)(2,1)}), bf16[64,18,512]{2,1,0:T(8,128)(2,1)S(1)}, u32[]{:S(2)}, u32[]{:S(2)}) %all-to-all-start) | async-done | bytes 1179680 | tf_op jit(solution)/shard_map/all_to_all | solution.py:134
  134.1 1.2 reshape.657
  135.3 5.0 %convolution_convert_fusion = bf16[1152,1536]{1,0:T(8,128)(2,1)} fusion(bf16[1152,512]{1,0:T(8,128)(2,1)} %reshape.657, bf16[512,1536]{1,0:T(8,128)(2,1)S(1)} %copy-done), kind=kOutput, calls=%fused_computation.255 | convolution fusion | flops 1813708800 | bytes 6291456 | tf_op jit(solution)/shard_map/dot_general | solution.py:137
  140.4 0.7 copy-done.7
  141.1 52.2 %all-gather.5.cloned.1.call-done = bf16[1024,1024]{1,0:T(8,128)(2,1)} async-done(((bf16[16,1024]{1,0:T(8,128)(2,1)}), bf16[1024,1024]{1,0:T(8,128)(2,1)}) %all-gather.5.cloned.1.call-update) | async-done | bytes 2097168 | tf_op jit(solution)/shard_map/all_gather | solution.py:18
  193.4 140.1 %all-gather.7.cloned.1.call-done = bf16[1024,1024]{1,0:T(8,128)(2,1)} async-done(((bf16[16,1024]{1,0:T(8,128)(2,1)}), bf16[1024,1024]{1,0:T(8,128)(2,1)}) %all-gather.7.cloned.1.call-update) | async-done | bytes 2097168 | tf_op jit(solution)/shard_map/all_gather | solution.py:18
  333.5 4.6 fusion.93
  338.0 1.3 convert_element_type.73
  339.4 57.4 %all-to-all-start.1 = ((bf16[64,18,512]{2,1,0:T(8,128)(2,1)}), bf16[64,18,512]{2,1,0:T(8,128)(2,1)}, u32[]{:S(2)}, u32[]{:S(2)}) async-start(bf16[64,18,512]{2,1,0:T(8,128)(2,1)} %convert_element_type.73), calls=%async_computation.1 | async-start | bytes 3145728 | tf_op jit(solution)/shard_map/all_to_all | solution.py:142
  396.8 12.9 %while.38 = (s32[]{:T(128)}, f32[16,1024]{1,0:T(8,128)S(1)}, f32[4,16,1024]{2,1,0:T(8,128)S(1)}, f32[4,16,1024]{2,1,0:T(8,128)}, f32[16,1024]{1,0:T(8,128)S(1)},...) while((s32[]{:T(128)}, f32[16,1024]{1,0:T(8,128)S(1)}, ...), condition=%wide.region_21.22_spmd, body=%wide.region_4.21_spmd.sunk | while | flops 2359313 | bytes 1940765 | solution.py:62
  396.8 0.2 fusion.124
  397.0 1.8 constant_dynamic-slice_fusion.114
  399.1 0.3 multiply_reduce_fusion.21
  399.5 0.1 multiply_reduce_fusion.24
  399.7 0.1 multiply_reduce_fusion.23
  400.0 0.2 fusion.124
  400.2 1.8 constant_dynamic-slice_fusion.114
  402.3 0.3 multiply_reduce_fusion.21
  402.8 0.1 multiply_reduce_fusion.24
  402.9 0.1 multiply_reduce_fusion.23
  403.2 0.2 fusion.124
  403.4 1.8 constant_dynamic-slice_fusion.114
  405.6 0.3 multiply_reduce_fusion.21
  406.0 0.1 multiply_reduce_fusion.24
  406.2 0.1 multiply_reduce_fusion.23
  406.5 0.2 fusion.124
  406.7 1.8 constant_dynamic-slice_fusion.114
  408.8 0.3 multiply_reduce_fusion.21
  409.4 0.1 multiply_reduce_fusion.23
  409.8 0.9 fusion.104
  410.7 54.4 %all-to-all-done.1 = bf16[64,18,512]{2,1,0:T(8,128)(2,1)} async-done(((bf16[64,18,512]{2,1,0:T(8,128)(2,1)}), bf16[64,18,512]{2,1,0:T(8,128)(2,1)}, u32[]{:S(2)}, u32[]{:S(2)}) %all-to-all-start.1) | async-done | bytes 1179680 | tf_op jit(solution)/shard_map/all_to_all | solution.py:142
  465.1 1.7 convert_reduce_fusion
  466.8 0.9 convolution_convert_fusion.2
  (198 shorter events, 3.8 us)
Async XLA Ops:
  8.0 127.3 %copy-start = (bf16[512,1536]{1,0:T(8,128)(2,1)S(1)}, bf16[512,1536]{1,0:T(8,128)(2,1)}, u32[]{:S(2)}) copy-start(bf16[512,1536]{1,0:T(8,128)(2,1)} %param.34) | copy-start | bytes 4718596
  8.0 185.3 %all-gather.5.cloned.1.call-start = ((), (), s32[]{:S(2)}) async-start(), calls=%async_computation.3 | async-start | bytes 2129920 | tf_op jit(solution)/shard_map/all_gather | solution.py:18
  8.9 8.0 %collective-permute-start = (bf16[3,1024]{1,0:T(4,128)(2,1)S(1)}, bf16[3,1024]{1,0:T(4,128)(2,1)S(1)}, u32[]{:S(2)}, u32[]{:S(2)}) collective-permute-start(bf16[3,1024]{1,0:T(4,128)(2,1)S(1)} %slice.515), channel_id=1, source_target_pairs={{0,8},{8,16},{16,24},{24,32},{32,40},{40,48},{48,56},{56,64},{64,7... | collective-permute-start | bytes 18440 | tf_op jit(solution)/shard_map/ppermute | solution.py:12
  18.7 5.0 %copy-start.9 = (s32[64,2]{0,1:T(2,128)S(1)}, s32[64,2]{0,1:T(2,128)}, u32[]{:S(2)}) copy-start(s32[64,2]{0,1:T(2,128)} %param.33) | copy-start | bytes 1540
  18.7 5.1 %copy-start.3 = (bf16[64,512]{1,0:T(8,128)(2,1)S(1)}, bf16[64,512]{1,0:T(8,128)(2,1)}, u32[]{:S(2)}) copy-start(bf16[64,512]{1,0:T(8,128)(2,1)} %param.31) | copy-start | bytes 196612
  18.7 5.0 %copy-start.10 = (bf16[512,8]{0,1:T(8,128)(2,1)S(1)}, bf16[512,8]{0,1:T(8,128)(2,1)}, u32[]{:S(2)}) copy-start(bf16[512,8]{0,1:T(8,128)(2,1)} %param.32) | copy-start | bytes 24580
  22.9 13.1 %copy-start.6 = (f32[16,1024]{1,0:T(8,128)}, f32[16,1024]{1,0:T(8,128)S(1)}, u32[]{:S(2)}) copy-start(f32[16,1024]{1,0:T(8,128)S(1)} %get-tuple-element.127) | copy-start | bytes 196612
  22.9 16.2 %copy-start.1 = (f32[4,16,1024]{2,1,0:T(8,128)}, f32[4,16,1024]{2,1,0:T(8,128)S(1)}, u32[]{:S(2)}) copy-start(f32[4,16,1024]{2,1,0:T(8,128)S(1)} %get-tuple-element.950) | copy-start | bytes 786436
  22.9 16.2 %copy-start.2 = (f32[4,16,1024]{2,1,0:T(8,128)}, f32[4,16,1024]{2,1,0:T(8,128)S(1)}, u32[]{:S(2)}) copy-start(f32[4,16,1024]{2,1,0:T(8,128)S(1)} %get-tuple-element.951) | copy-start | bytes 786436
  39.1 95.0 %all-to-all-start = ((bf16[64,18,512]{2,1,0:T(8,128)(2,1)}), bf16[64,18,512]{2,1,0:T(8,128)(2,1)S(1)}, u32[]{:S(2)}, u32[]{:S(2)}) async-start(bf16[64,18,512]{2,1,0:T(8,128)(2,1)} %bitcast.98), calls=%async_computation | async-start | bytes 3145728 | tf_op jit(solution)/shard_map/all_to_all | solution.py:134
  55.6 277.8 %all-gather.7.cloned.1.call-start = ((), (), s32[]{:S(2)}) async-start(), calls=%async_computation.4 | async-start | bytes 2129920 | tf_op jit(solution)/shard_map/all_gather | solution.py:18
  57.1 276.3 %all-reduce.2.cloned.1.call-start = ((), (), s32[]{:S(2)}) async-start(), calls=%async_computation.2 | async-start | bytes 7077888 | tf_op jit(solution)/shard_map/psum | solution.py:138
  140.3 0.7 copy-start.7
  339.4 125.7 %all-to-all-start.1 = ((bf16[64,18,512]{2,1,0:T(8,128)(2,1)}), bf16[64,18,512]{2,1,0:T(8,128)(2,1)}, u32[]{:S(2)}, u32[]{:S(2)}) async-start(bf16[64,18,512]{2,1,0:T(8,128)(2,1)} %convert_element_type.73), calls=%async_computation.1 | async-start | bytes 3145728 | tf_op jit(solution)/shard_map/all_to_all | solution.py:142
  396.8 13.0 %copy-start.5 = (bf16[64,1024]{1,0:T(8,128)(2,1)S(1)}, bf16[64,1024]{1,0:T(8,128)(2,1)}, u32[]{:S(2)}) copy-start(bf16[64,1024]{1,0:T(8,128)(2,1)} %param.22) | copy-start | bytes 393220
  396.8 13.0 %copy-start.8 = (f32[1024]{0:T(1024)S(1)}, f32[1024]{0:T(1024)}, u32[]{:S(2)}) copy-start(f32[1024]{0:T(1024)} %param.28) | copy-start | bytes 12292
  396.8 13.0 %copy-start.11 = (f32[1024]{0:T(1024)S(1)}, f32[1024]{0:T(1024)}, u32[]{:S(2)}) copy-start(f32[1024]{0:T(1024)} %param.29) | copy-start | bytes 12292
  409.7 57.1 %copy-start.4 = (f32[144,64]{0,1:T(8,128)S(1)}, f32[144,64]{0,1:T(8,128)}, u32[]{:S(2)}) copy-start(f32[144,64]{0,1:T(8,128)} %get-tuple-element.170) | copy-start | bytes 110596
Sparse Core Ops, SparseCore 0:
  23.8 169.5 all-gather.4
  196.3 137.1 all-gather.6
Sparse Core Ops, SparseCore 1:
  140.5 76.9 all-reduce.1
where the time goes:
time: 481 us; the launch traced here: 475 us
  waiting for transfers between devices  324 us (67%)
  starting transfers between devices  77.4 us (16%)
  local copies, waits for them, and re-layouts  18 us (4%)
  between operations  15.8 us (3%)
  other arithmetic  14.6 us (3%)
  matrix products  12.2 us (3%)
  blocking collectives  12.1 us (3%)
    all_gather x2, waiting for transfers between devices, carried_in(): lax.all_gather(a.astype(kind), axis)  192 us
    all_to_all x1, waiting for transfers between devices, local(): lax.all_to_all(outgoing, 'seq', split_axis=0, concat_axis=0, tiled=True)  76.9 us
    all_to_all x1, starting transfers between devices, local(): lax.all_to_all(produced.astype(jnp.bfloat16), 'seq', split_axis=0, concat...  57.4 us
    all_to_all x1, waiting for transfers between devices, local(): lax.all_to_all(produced.astype(jnp.bfloat16), 'seq', split_axis=0, concat...  54.4 us
    all_to_all x1, starting transfers between devices, local(): lax.all_to_all(outgoing, 'seq', split_axis=0, concat_axis=0, tiled=True)  16.5 us
    psum x1, blocking collectives, local(): lax.psum(jnp.dot(hidden, router, preferred_element_type=jnp.float32), 'exp')  12.1 us
  transfers between devices with their start and end apart: 6, of which 4 were waited for; matrix products, arithmetic and copies ran while one was open for 6% of the time, Pallas kernels for 0%

commit v1 on v0

--- a/solution.py
+++ b/solution.py
@@ -1,9 +1,329 @@
+import functools
+
 import jax
 import jax.numpy as jnp
 from jax import lax
+from jax.experimental import pallas as pl
+from jax.experimental.pallas import tpu as pltpu
 from jax.sharding import PartitionSpec as P
 
 CAP = 18
+PAD = 32
+NZ, NY, NX = 16, 4, 4
+MESH = pl.DeviceIdType.MESH
+BF, F32 = jnp.bfloat16, jnp.float32
+BATCHES = 4
+
+
+def dot(a, b):
+    return jnp.dot(a, b, preferred_element_type=F32)
+
+
+class Mail:
+    def __init__(self, send, recv):
+        self.send, self.recv, self.count, self.sent = send, recv, 0, []
+
+    def post(self, src, dst, slot, to, unless=None):
+        copy = pltpu.make_async_remote_copy(
+            src_ref=src, dst_ref=dst, send_sem=self.send.at[self.count], recv_sem=self.recv.at[slot],
+            device_id=to, device_id_type=MESH)
+        self.count += 1
+        self.sent.append((copy, unless))
+        if unless is None:
+            copy.start()
+        else:
+            pl.when(jnp.logical_not(unless))(copy.start)
+
+    def take(self, dst, slot, unless=None):
+        copy = pltpu.make_async_remote_copy(
+            src_ref=dst, dst_ref=dst, send_sem=self.send.at[0], recv_sem=self.recv.at[slot],
+            device_id=(lax.axis_index("seq"), lax.axis_index("exp")), device_id_type=MESH)
+        if unless is None:
+            copy.wait_recv()
+        else:
+            pl.when(jnp.logical_not(unless))(copy.wait_recv)
+
+    def finish(self):
+        for copy, unless in self.sent:
+            if unless is None:
+                copy.wait_send()
+            else:
+                pl.when(jnp.logical_not(unless))(copy.wait_send)
+
+
+def expert_kernel(hid, router_t, ids_t, wg_in, wd_in, out,
+                  wg, wd, pack, in1, rt, sbuf, rbuf, act, prod, ys, yc, zs, zr, back, ret, lgs, lgr,
+                  send, recv, local):
+    seq, exp = lax.axis_index("seq"), lax.axis_index("exp")
+    z, y, x, c = seq // NY, lax.rem(seq, NY), exp // 2, lax.rem(exp, 2)
+    half = lax.rem(z, 2)
+    zpair = z + 1 - 2 * half
+    near = {1: lax.rem(y + 1, NY), -1: lax.rem(y + NY - 1, NY)}
+    xs = {d: lax.rem(x + d + NX, NX) for d in (-1, 0, 1, 2)}
+    ff = wg.shape[3]
+
+    def at(z_, y_, x_, c_):
+        return (z_ * NY + y_, x_ * 2 + c_)
+
+    mate = at(z, y, x, 1 - c)
+    ypeer = {d: at(z, near[d], x, c) for d in (1, -1)}
+    xpeer = {d: at(z, y, xs[d], c) for d in (1, -1)}
+    zpeer = at(zpair, y, x, c)
+    experts = 8
+
+    barrier = pltpu.get_barrier_semaphore()
+    home = half == c
+
+    def greet(to):
+        pl.semaphore_signal(barrier, inc=1, device_id=to, device_id_type=MESH)
+
+    order = [4, 3, 5, 2, 6, 1, 7, 0]
+    groups = [lax.rem(z // 2 + off, experts) for off in order]
+    for e, off in zip(groups, order):
+        to = at(2 * e + c, y, x, half)
+        if off == 0:
+            pl.when(jnp.logical_not(home))(functools.partial(greet, to))
+        else:
+            greet(to)
+    for to in (zpeer, ypeer[1], ypeer[-1]):
+        greet(to)
+    for j in range(1, 8):
+        greet((seq, lax.rem(exp + j, 8)))
+
+    loads = []
+    for q in range(NX):
+        loads.append(pltpu.make_async_copy(wg_in.at[:, pl.ds(q * ff, ff)], wg.at[c, q], local.at[q]))
+    loads.append(pltpu.make_async_copy(wd_in, wd.at[c], local.at[NX]))
+    for copy in loads:
+        copy.start()
+
+    ids = ids_t[...]
+    tokens = ids.shape[1]
+    e_iota = lax.broadcasted_iota(jnp.int32, (experts, tokens), 0)
+    hits = [(ids[k:k + 1, :] == e_iota).astype(F32) for k in range(2)]
+    ahead = (lax.broadcasted_iota(jnp.int32, (tokens, tokens), 0)
+             < lax.broadcasted_iota(jnp.int32, (tokens, tokens), 1)).astype(BF)
+    before = dot((hits[0] + hits[1]).astype(BF), ahead)
+    keys = [ids[k:k + 1, :] * PAD + jnp.sum(hits[k] * before, axis=0, keepdims=True).astype(jnp.int32)
+            for k in range(2)]
+    r_iota = lax.broadcasted_iota(jnp.int32, (experts * PAD, tokens), 0)
+    match = [r_iota == keys[k] for k in range(2)]
+    selector = jnp.where(match[0] | match[1], 1.0, 0.0).astype(BF)
+    h = hid[...]
+    pack[...] = dot(selector, h).astype(BF).reshape(pack.shape)
+    lg = lax.dot_general(router_t[...], h, (((1,), (1,)), ((), ())), preferred_element_type=F32)
+    lgs[...] = jnp.concatenate([lg, jnp.zeros((experts, 128 - tokens), F32)], axis=1)
+    rows = CAP * experts
+    r_c = lax.broadcasted_iota(jnp.int32, (rows, experts * PAD), 0)
+    q_c = lax.broadcasted_iota(jnp.int32, (rows, experts * PAD), 1)
+    group = sum((r_c >= CAP * m).astype(jnp.int32) for m in range(1, experts))
+    tight = jnp.where(q_c == r_c + (PAD - CAP) * group, 1.0, 0.0).astype(BF)
+    q_e = lax.broadcasted_iota(jnp.int32, (experts * PAD, rows), 0)
+    r_e = lax.broadcasted_iota(jnp.int32, (experts * PAD, rows), 1)
+    group_e = sum((r_e >= CAP * m).astype(jnp.int32) for m in range(1, experts))
+    loose = jnp.where(q_e == r_e + (PAD - CAP) * group_e, 1.0, 0.0).astype(BF)
+
+    mail = Mail(send, recv)
+    pl.semaphore_wait(barrier, 8 + 3 + 7 - home.astype(jnp.int32))
+
+    IN1, RT, RS, ACT = 0, 8, 16, 28
+    YS, YC, ZR, RET, LG, WG, WD = 44, 46, 48, 49, 57, 65, 69
+
+    for e, off in zip(groups, order):
+        mail.post(pack.at[e], in1.at[z // 2], IN1 + z // 2, at(2 * e + c, y, x, half),
+                  home if off == 0 else None)
+    own_group = z // 2
+    stay = pltpu.make_async_copy(pack.at[own_group], in1.at[own_group], local.at[NX + 1])
+    pl.when(home)(stay.start)
+    for q in range(NX):
+        mail.post(wg_in.at[:, pl.ds(q * ff, ff)], wg.at[c, q], WG + q, mate)
+    mail.post(wd_in, wd.at[c], WD, mate)
+    for j in range(1, 8):
+        mail.post(lgs, lgr.at[exp], LG + exp, (seq, lax.rem(exp + j, 8)))
+    pl.when(home)(stay.wait)
+    for e, off in zip(groups, order):
+        mail.take(in1.at[e], IN1 + e, home if off == 0 else None)
+
+    rt[0, half] = dot(tight, in1[...].reshape(experts * PAD, -1)).astype(BF)
+    other = 1 - half
+    mail.post(rt.at[0, half], rt.at[0, half], RT + half, zpeer)
+    mail.post(rt.at[0, half], rt.at[2, half], RT + 4 + half, ypeer[1])
+    mail.post(rt.at[0, half], rt.at[1, half], RT + 2 + half, ypeer[-1])
+    mail.take(rt.at[0, other], RT + other)
+    mail.post(rt.at[0, other], rt.at[2, other], RT + 4 + other, ypeer[1])
+    mail.post(rt.at[0, other], rt.at[1, other], RT + 2 + other, ypeer[-1])
+    for copy in loads:
+        copy.wait()
+    for q in range(NX):
+        mail.take(wg.at[1 - c, q], WG + q)
+
+    def gathered(k):
+        if k == 1:
+            mail.take(rt.at[1, 1], RT + 3)
+            mail.post(rt.at[1, 1], rt.at[3, 1], RT + 7, ypeer[-1])
+            mail.take(rt.at[1, 0], RT + 2)
+        elif k == 2:
+            mail.take(rt.at[2, 0], RT + 4)
+            mail.post(rt.at[2, 0], rt.at[3, 0], RT + 6, ypeer[1])
+            mail.take(rt.at[2, 1], RT + 5)
+        elif k == 3:
+            mail.take(rt.at[3, 0], RT + 6)
+            mail.take(rt.at[3, 1], RT + 7)
+
+    def part(k, q):
+        return dot(rt[k, 0], wg[0, q]) + dot(rt[k, 1], wg[1, q])
+
+    way = [1 if k % 2 == 0 else -1 for k in range(BATCHES)]
+    kept = {}
+
+    def first(k):
+        d = way[k]
+        sbuf[k, 0] = part(k, xs[2]).astype(BF)
+        mail.post(sbuf.at[k, 0], rbuf.at[k, 0], RS + 3 * k, xpeer[d])
+        sbuf[k, 1] = part(k, xs[-d]).astype(BF)
+        mail.post(sbuf.at[k, 1], rbuf.at[k, 1], RS + 3 * k + 1, xpeer[-d])
+        sbuf[k, 2] = part(k, xs[d]).astype(BF)
+        sbuf[k, 3] = part(k, x).astype(BF)
+
+    def second(k):
+        d = way[k]
+        mail.take(rbuf.at[k, 0], RS + 3 * k)
+        sbuf[k, 4] = (sbuf[k, 2].astype(F32) + rbuf[k, 0].astype(F32)).astype(BF)
+        mail.post(sbuf.at[k, 4], rbuf.at[k, 2], RS + 3 * k + 2, xpeer[d])
+
+    def third(k):
+        mail.take(rbuf.at[k, 1], RS + 3 * k + 1)
+        mail.take(rbuf.at[k, 2], RS + 3 * k + 2)
+        total = sbuf[k, 3].astype(F32) + rbuf[k, 1].astype(F32) + rbuf[k, 2].astype(F32)
+        act[k, x] = jax.nn.silu(total).astype(BF)
+        for d in (1, -1):
+            mail.post(act.at[k, x], act.at[k, x], ACT + 4 * k + x, xpeer[d])
+
+    def fourth(k):
+        d = way[k]
+        mail.take(act.at[k, xs[-d]], ACT + 4 * k + xs[-d])
+        mail.post(act.at[k, xs[-d]], act.at[k, xs[-d]], ACT + 4 * k + xs[-d], xpeer[d])
+
+    def down(k):
+        d = way[k]
+        mail.take(act.at[k, xs[d]], ACT + 4 * k + xs[d])
+        mail.take(act.at[k, xs[2]], ACT + 4 * k + xs[2])
+        for f in range(2):
+            total = dot(act[k, 0], wd[f, 0:ff])
+            for q in range(1, NX):
+                total += dot(act[k, q], wd[f, q * ff:(q + 1) * ff])
+            prod[k, f] = total.astype(BF)
+
+    steps = [("g", 0), ("a", 0), ("g", 1), ("g", 2), ("a", 1), ("b", 0), ("a", 2), ("b", 1), ("c", 0), ("g", 3),
+             ("a", 3), ("b", 2), ("c", 1), ("d", 0), ("b", 3), ("c", 2), ("d", 1), ("w", 0), ("e", 0), ("c", 3),
+             ("d", 2), ("e", 1), ("d", 3), ("e", 2), ("e", 3)]
+    for what, k in steps:
+        if what == "g":
+            gathered(k)
+        elif what == "a":
+            first(k)
+        elif what == "b":
+            second(k)
+        elif what == "c":
+            third(k)
+        elif what == "d":
+            fourth(k)
+        elif what == "w":
+            mail.take(wd.at[1 - c], WD)
+        else:
+            down(k)
+
+    mail.post(prod.at[3, 0], yc.at[0], YC, ypeer[1])
+    mail.post(prod.at[3, 1], yc.at[1], YC + 1, ypeer[-1])
+    mail.post(prod.at[1, 1], ys.at[1], YS + 1, ypeer[1])
+    mail.post(prod.at[2, 0], ys.at[0], YS, ypeer[-1])
+    mail.take(yc.at[0], YC)
+    zs[0] = (prod[1, 0].astype(F32) + yc[0].astype(F32)).astype(BF)
+    mail.post(zs.at[0], yc.at[2], RET + 21, ypeer[1])
+    mail.take(yc.at[1], YC + 1)
+    zs[1] = (prod[2, 1].astype(F32) + yc[1].astype(F32)).astype(BF)
+    mail.post(zs.at[1], yc.at[3], RET + 22, ypeer[-1])
+    mail.take(ys.at[0], YS)
+    mail.take(ys.at[1], YS + 1)
+    mail.take(yc.at[2], RET + 21)
+    mail.take(yc.at[3], RET + 22)
+
+    def over_y(f):
+        return prod[0, f].astype(F32) + ys[f].astype(F32) + yc[2 + f].astype(F32)
+
+    zs[2] = over_y(other).astype(BF)
+    mail.post(zs.at[2], zr, ZR, zpeer)
+    mine = over_y(half)
+    mail.take(zr, ZR)
+    final = (mine + zr[...].astype(F32)).astype(BF)
+    back[...] = dot(loose, final).astype(BF).reshape(back.shape)
+
+    for i, off in zip(groups, order):
+        mail.post(back.at[i], ret.at[own_group], RET + own_group, at(2 * i + c, y, x, half),
+                  home if off == 0 else None)
+    last = pltpu.make_async_copy(back.at[own_group], ret.at[own_group], local.at[NX + 2])
+    pl.when(home)(last.start)
+
+    for j in range(1, 8):
+        q = lax.rem(exp + j, 8)
+        mail.take(lgr.at[q], LG + q)
+    lgr[exp] = lgs[...]
+    logits = lgr[0]
+    for q in range(1, 8):
+        logits += lgr[q]
+    logits = logits[:, :tokens]
+    picked = [jnp.sum(hits[k] * logits, axis=0, keepdims=True) for k in range(2)]
+    gates = [jax.nn.sigmoid(picked[0] - picked[1]), jax.nn.sigmoid(picked[1] - picked[0])]
+    blend = jnp.where(match[0], gates[0], 0.0) + jnp.where(match[1], gates[1], 0.0)
+    upper = blend.astype(BF)
+    lower = (blend - upper.astype(F32)).astype(BF)
+
+    pl.when(home)(last.wait)
+    for e, off in zip(groups, order):
+        mail.take(ret.at[e], RET + e, home if off == 0 else None)
+    rows_in = ret[...].reshape(experts * PAD, -1)
+    turn = (((0,), (0,)), ((), ()))
+    out[...] = (lax.dot_general(upper, rows_in, turn, preferred_element_type=F32)
+                + lax.dot_general(lower, rows_in, turn, preferred_element_type=F32)).astype(BF)
+    mail.finish()
+
+
+def experts_of(hidden, router, expert_ids, w_gate, w_down):
+    tokens, feats = hidden.shape
+    rows, ff = CAP * 8, w_gate.shape[1] // NX
+    vm = pl.BlockSpec(memory_space=pltpu.VMEM)
+    hbm = pl.BlockSpec(memory_space=pl.ANY)
+    return pl.pallas_call(
+        expert_kernel,
+        out_shape=jax.ShapeDtypeStruct((tokens, feats), BF),
+        in_specs=[vm, vm, vm, hbm, hbm],
+        out_specs=vm,
+        scratch_shapes=[
+            pltpu.VMEM((2, NX, feats, ff), BF),
+            pltpu.VMEM((2, NX * ff, feats), BF),
+            pltpu.VMEM((8, PAD, feats), BF),
+            pltpu.VMEM((8, PAD, feats), BF),
+            pltpu.VMEM((BATCHES, 2, rows, feats), BF),
+            pltpu.VMEM((BATCHES, 5, rows, ff), BF),
+            pltpu.VMEM((BATCHES, 3, rows, ff), BF),
+            pltpu.VMEM((BATCHES, NX, rows, ff), BF),
+            pltpu.VMEM((BATCHES, 2, rows, feats), BF),
+            pltpu.VMEM((2, rows, feats), BF),
+            pltpu.VMEM((4, rows, feats), BF),
+            pltpu.VMEM((3, rows, feats), BF),
+            pltpu.VMEM((rows, feats), BF),
+            pltpu.VMEM((8, PAD, feats), BF),
+            pltpu.VMEM((8, PAD, feats), BF),
+            pltpu.VMEM((8, 128), F32),
+            pltpu.VMEM((8, 8, 128), F32),
+            pltpu.SemaphoreType.DMA((96,)),
+            pltpu.SemaphoreType.DMA((96,)),
+            pltpu.SemaphoreType.DMA((8,)),
+        ],
+        compiler_params=pltpu.CompilerParams(collective_id=0, has_side_effects=True,
+                                             vmem_limit_bytes=60 * 1024 * 1024),
+        name="experts",
+    )(hidden, router.T, expert_ids.T, w_gate, w_down)
 
 
 def passed_along(value, axis, steps):
@@ -109,44 +429,8 @@
     mamba_out = (
         (readout + d_skip[None, :] * activated) * jax.nn.silu(z_gate.astype(jnp.float32))
     ).astype(jnp.bfloat16)
-    experts = router.shape[1]
-    picks = expert_ids.shape[1]
-    feature_width = hidden.shape[1]
-    group_size = lax.axis_size("seq") // experts
-    logits = lax.psum(jnp.dot(hidden, router, preferred_element_type=jnp.float32), "exp")
-    expert_iota = lax.broadcasted_iota(jnp.int32, (1, 1, experts), 2)
-    chosen = expert_ids[:, :, None] == expert_iota
-    picked = jnp.sum(jnp.where(chosen, logits[:, None, :], 0.0), axis=2)
-    gates = jax.nn.sigmoid(picked - picked[:, ::-1])
-    flat_hits = chosen.reshape(tok_rows * picks, experts).astype(jnp.int32)
-    earlier_hits = jnp.cumsum(flat_hits, axis=0) - flat_hits
-    slots = jnp.sum(earlier_hits * flat_hits, axis=1).reshape(tok_rows, picks)
-    slot_keys = expert_ids * CAP + slots
-    slot_iota = lax.broadcasted_iota(jnp.int32, (experts * CAP, 1, 1), 0)
-    matches = slot_keys[None] == slot_iota
-    selector = jnp.sum(matches.astype(jnp.float32), axis=2).astype(jnp.bfloat16)
-    blending = jnp.sum(jnp.where(matches, gates[None], 0.0), axis=2)
-    packed = jnp.dot(selector, hidden, preferred_element_type=jnp.float32).astype(jnp.bfloat16)
-    outgoing = jnp.broadcast_to(
-        packed.reshape(experts, 1, CAP, feature_width), (experts, group_size, CAP, feature_width)
-    )
-    outgoing = outgoing.reshape(experts * group_size, CAP, feature_width)
-    arrived = lax.all_to_all(outgoing, "seq", split_axis=0, concat_axis=0, tiled=True)
-    sources, entries, features = arrived.shape
-    routed = arrived.reshape(sources * entries, features)
-    partial_value = jnp.dot(routed, w_gate, preferred_element_type=jnp.float32)
-    summed = lax.psum(partial_value.astype(jnp.bfloat16), "exp").astype(jnp.float32)
-    acted = jax.nn.silu(summed).astype(jnp.bfloat16)
-    produced = jnp.dot(acted, w_down, preferred_element_type=jnp.float32)
-    produced = produced.reshape(sources, entries, features)
-    returned = lax.all_to_all(
-        produced.astype(jnp.bfloat16), "seq", split_axis=0, concat_axis=0, tiled=True
-    ).astype(produced.dtype)
-    combined = jnp.sum(returned.reshape(experts, group_size, CAP, feature_width), axis=1).reshape(
-        experts * CAP, feature_width
-    )
-    moe_out = jnp.einsum("rt,rd->td", blending, combined, precision=lax.Precision.HIGHEST)
-    return (mamba_out, moe_out.astype(jnp.bfloat16))
+    moe_out = experts_of(hidden, router, expert_ids, w_gate, w_down)
+    return (mamba_out, moe_out)
 
 
 def solution(mesh):

time: 481 us -> 371 us (0.77)
  the two profiles are of different devices: /device:TPU:6 before, /device:TPU:504 now
where the time goes in v1:
time: 371 us; the launch traced here: 366 us
  waiting for transfers between devices  189 us (51%)
  Pallas kernels  89.7 us (24%)
  other arithmetic  61.1 us (16%)
  between operations  14.2 us (4%)
  local copies, waits for them, and re-layouts  6.69 us (2%)
    all_gather x2, waiting for transfers between devices, carried_in(): lax.all_gather(a.astype(kind), axis)  188 us
    pallas_call x1, Pallas kernels, experts_of(): pl.pallas_call(expert_kernel, out_shape=jax.ShapeDtypeStruct((tokens, fea...  89.7 us
    add x63, other arithmetic, link_pairs(): return (earlier[0] * later[0], later[0] * earlier[1] + later[1])  50.3 us
  transfers between devices with their start and end apart: 3, of which 3 were waited for; matrix products, arithmetic and copies ran while one was open for 1% of the time, Pallas kernels for 25%

profile of v1, /device:TPU:504, one launch (start us, length us, event | category | flops | bytes accessed | tf_op | source)
XLA Modules:
  0.0 366.0 jit_solution(15570578487212906809)
XLA Ops:
  8.0 1.3 collective-permute-start
  9.3 0.9 fusion.96
  10.2 0.9 exponential_negate_fusion
  11.0 1.1 compare_select_fusion
  13.5 0.9 maximum_convert_fusion
  14.5 0.9 divide_multiply_fusion
  15.3 4.2 %while.39 = (s32[]{:T(128)}, f32[16,1024]{1,0:T(8,128)S(1)}, f32[16,1024]{1,0:T(8,128)S(1)}, f32[4,16,1024]{2,1,0:T(8,128)S(1)}, f32[16,1024]{1,0:T(8,128)S(1)},...) while((s32[]{:T(128)}, f32[16,1024]{1,0:T(8,128)S(1)}, ...), condition=%wide.region_1.2_spmd.clone, body=%wide.region_0.1_spmd.clone.sunk | while | flops 1622034 | bytes 1052180 | solution.py:382
  21.0 89.7 %experts.1 = bf16[64,512]{1,0:T(8,128)(2,1)} custom-call(bf16[64,512]{1,0:T(8,128)(2,1)} %hid.1, bf16[8,512]{1,0:T(8,128)(2,1)} %bitcast.536, s32[2,64]{1,0:T(2,128)} %bitcast.537, bf16[512,1536]{1,0:T(8,128)(2,1)} %wg_in.1, bf16[1536,512]{1,0:T(8,128)(2,1)} %wd_in.1), custom_call_target="tpu_custom_call" | custom-call | tf_op jit(solution)/shard_map/experts/pallas_call | solution.py:296
  110.7 48.1 %all-gather.5.cloned.1.call-done = bf16[1024,1024]{1,0:T(8,128)(2,1)} async-done(((bf16[16,1024]{1,0:T(8,128)(2,1)}), bf16[1024,1024]{1,0:T(8,128)(2,1)}) %all-gather.5.cloned.1.call-update) | async-done | bytes 2097168 | tf_op jit(solution)/shard_map/all_gather | solution.py:338
  158.8 140.3 %all-gather.7.cloned.1.call-done = bf16[1024,1024]{1,0:T(8,128)(2,1)} async-done(((bf16[16,1024]{1,0:T(8,128)(2,1)}), bf16[1024,1024]{1,0:T(8,128)(2,1)}) %all-gather.7.cloned.1.call-update) | async-done | bytes 2097168 | tf_op jit(solution)/shard_map/all_gather | solution.py:338
  299.1 51.8 %while.37 = (s32[]{:T(128)}, f32[16,1024]{1,0:T(8,128)S(1)}, s32[]{:T(128)}, bf16[64,16,1024]{2,1,0:T(8,128)(2,1)}, bf16[64,16,1024]{2,1,0:T(8,128)(2,1)}, /*index=5*/s32[]{:T(128)}, s32[]{:T(128)}, s32[]{:T(128)}) while((s32[]{:T(128)}, f32[16,1024]{1,0:T(8,128)S(1)}, s32[]{:T(128)}, bf16[64,16,1024]{2,1,0:T(8,128)(2,1)}, ...), condition=%wide.region_3.4_spmd, body=%wide.region_2.3_spmd.sunk | while | flops 65541 | bytes 196731 | solution.py:352
  299.9 0.8 convert_add_fusion.2
  300.7 0.8 convert_add_fusion.2
  301.5 0.8 convert_add_fusion.2
  302.4 0.8 convert_add_fusion.2
  303.2 0.8 convert_add_fusion.2
  304.0 0.8 convert_add_fusion.2
  304.8 0.8 convert_add_fusion.2
  305.7 0.8 convert_add_fusion.2
  306.5 0.8 convert_add_fusion.2
  307.3 0.8 convert_add_fusion.2
  308.1 0.8 convert_add_fusion.2
  309.0 0.8 convert_add_fusion.2
  309.8 0.8 convert_add_fusion.2
  310.6 0.8 convert_add_fusion.2
  311.4 0.8 convert_add_fusion.2
  312.2 0.8 convert_add_fusion.2
  313.1 0.8 convert_add_fusion.2
  313.9 0.8 convert_add_fusion.2
  314.7 0.8 convert_add_fusion.2
  315.5 0.8 convert_add_fusion.2
  317.2 0.8 convert_add_fusion.2
  318.0 0.8 convert_add_fusion.2
  318.8 0.8 convert_add_fusion.2
  319.7 0.8 convert_add_fusion.2
  320.5 0.8 convert_add_fusion.2
  321.3 0.8 convert_add_fusion.2
  322.1 0.8 convert_add_fusion.2
  325.4 0.8 convert_add_fusion.2
  326.2 0.8 convert_add_fusion.2
  327.1 0.8 convert_add_fusion.2
  327.9 0.8 convert_add_fusion.2
  328.7 0.8 convert_add_fusion.2
  329.5 0.8 convert_add_fusion.2
  330.4 0.8 convert_add_fusion.2
  332.8 0.8 convert_add_fusion.2
  333.7 0.8 convert_add_fusion.2
  334.5 0.8 convert_add_fusion.2
  335.3 0.8 convert_add_fusion.2
  336.1 0.8 convert_add_fusion.2
  336.9 0.8 convert_add_fusion.2
  337.8 0.8 convert_add_fusion.2
  341.1 0.8 convert_add_fusion.2
  341.9 0.8 convert_add_fusion.2
  342.7 0.8 convert_add_fusion.2
  343.5 0.8 convert_add_fusion.2
  344.4 0.8 convert_add_fusion.2
  345.2 0.8 convert_add_fusion.2
  346.0 0.8 convert_add_fusion.2
  348.5 0.8 convert_add_fusion.2
  349.3 0.8 convert_add_fusion.2
  350.1 0.8 convert_add_fusion.2
  351.0 6.6 %while.38 = (s32[]{:T(128)}, f32[16,1024]{1,0:T(8,128)S(1)}, f32[4,16,1024]{2,1,0:T(8,128)S(1)}, f32[4,16,1024]{2,1,0:T(8,128)S(1)}, f32[16,1024]{1,0:T(8,128)S(...) while((s32[]{:T(128)}, f32[16,1024]{1,0:T(8,128)S(1)}, ...), condition=%wide.region_21.22_spmd, body=%wide.region_4.21_spmd.sunk | while | flops 2359313 | bytes 1940757 | solution.py:382
  357.7 0.9 fusion.95
  (218 shorter events, 23.4 us)
Async XLA Ops:
  7.2 3.9 %copy-start = (bf16[256,1024]{1,0:T(8,128)(2,1)S(1)}, bf16[256,1024]{1,0:T(8,128)(2,1)}, u32[]{:S(2)}) copy-start(bf16[256,1024]{1,0:T(8,128)(2,1)} %param.24) | copy-start | bytes 1572868
  7.2 151.6 %all-gather.5.cloned.1.call-start = ((), (), s32[]{:S(2)}) async-start(), calls=%async_computation | async-start | bytes 2129920 | tf_op jit(solution)/shard_map/all_gather | solution.py:338
  8.0 5.5 %collective-permute-start = (bf16[3,1024]{1,0:T(4,128)(2,1)S(1)}, bf16[3,1024]{1,0:T(4,128)(2,1)S(1)}, u32[]{:S(2)}, u32[]{:S(2)}) collective-permute-start(bf16[3,1024]{1,0:T(4,128)(2,1)S(1)} %slice.515), channel_id=1, source_target_pairs={{0,8},{8,16},{16,24},{24,32},{32,40},{40,48},{48,56},{56,64},{64,7... | collective-permute-start | bytes 18440 | tf_op jit(solution)/shard_map/ppermute | solution.py:332
  20.2 278.9 %all-gather.7.cloned.1.call-start = ((), (), s32[]{:S(2)}) async-start(), calls=%async_computation.1 | async-start | bytes 2129920 | tf_op jit(solution)/shard_map/all_gather | solution.py:338
  350.9 6.7 %copy-start.2 = (bf16[64,1024]{1,0:T(8,128)(2,1)S(1)}, bf16[64,1024]{1,0:T(8,128)(2,1)}, u32[]{:S(2)}) copy-start(bf16[64,1024]{1,0:T(8,128)(2,1)} %param.22) | copy-start | bytes 393220
  350.9 6.7 %copy-start.3 = (f32[1024]{0:T(1024)S(1)}, f32[1024]{0:T(1024)}, u32[]{:S(2)}) copy-start(f32[1024]{0:T(1024)} %param.28) | copy-start | bytes 12292
  351.0 6.7 %copy-start.4 = (f32[1024]{0:T(1024)S(1)}, f32[1024]{0:T(1024)}, u32[]{:S(2)}) copy-start(f32[1024]{0:T(1024)} %param.29) | copy-start | bytes 12292
  351.0 7.6 %copy-start.1 = (bf16[64,512]{1,0:T(8,128)(2,1)S(1)}, bf16[64,512]{1,0:T(8,128)(2,1)}, u32[]{:S(2)}) copy-start(bf16[64,512]{1,0:T(8,128)(2,1)} %experts.1) | copy-start | bytes 196612
Sparse Core Ops, SparseCore 0:
  20.3 138.4 all-gather.4
  162.3 136.7 all-gather.6

commit v2 on v1

--- a/solution.py
+++ b/solution.py
@@ -51,9 +51,11 @@
                 pl.when(jnp.logical_not(unless))(copy.wait_send)
 
 
-def expert_kernel(hid, router_t, ids_t, wg_in, wd_in, out,
-                  wg, wd, pack, in1, rt, sbuf, rbuf, act, prod, ys, yc, zs, zr, back, ret, lgs, lgr,
-                  send, recv, local):
+def layer_kernel(x_in, z_gate, dt_low, dt_weight, dt_bias, a_log, conv_weight, conv_bias, d_skip, b_and_c,
+                 hid, router_t, ids_t, wg_in, wd_in, mixed, out,
+                 wg, wd, pack, in1, rt, sbuf, rbuf, act, prod, ys, yc, zs, zr, back, ret, lgs, lgr,
+                 tail, padded, active, delta, drive, rates, factor, state, rowend, rowall, zall, entry, reads,
+                 send, recv, local):
     seq, exp = lax.axis_index("seq"), lax.axis_index("exp")
     z, y, x, c = seq // NY, lax.rem(seq, NY), exp // 2, lax.rem(exp, 2)
     half = lax.rem(z, 2)
@@ -89,6 +91,16 @@
         greet(to)
     for j in range(1, 8):
         greet((seq, lax.rem(exp + j, 8)))
+    yfar = lax.rem(y + 2, NY)
+    greet(at(z, yfar, x, c))
+    starts, ends = seq == 0, seq == NZ * NY - 1
+    pl.when(jnp.logical_not(starts))(functools.partial(greet, (seq - jnp.where(starts, 0, 1), exp)))
+
+    def greet_earlier(other_z, carry):
+        greet(at(other_z, y, x, c))
+        return carry
+
+    lax.fori_loop(0, z, greet_earlier, 0)
 
     loads = []
     for q in range(NX):
@@ -123,15 +135,28 @@
     group_e = sum((r_e >= CAP * m).astype(jnp.int32) for m in range(1, experts))
     loose = jnp.where(q_e == r_e + (PAD - CAP) * group_e, 1.0, 0.0).astype(BF)
 
+    channels = x_in.shape[1]
+    tiles = channels // 128
+
+    def tiled(ref, values):
+        for j in range(tiles):
+            ref[:, j, :] = values[:, j * 128:(j + 1) * 128]
+
+    step = jax.nn.softplus(dot(dt_low[...], dt_weight[...]) + dt_bias[...])
+    tiled(delta, step)
+    tiled(rates, -jnp.exp(a_log[...]))
+
     mail = Mail(send, recv)
-    pl.semaphore_wait(barrier, 8 + 3 + 7 - home.astype(jnp.int32))
+    pl.semaphore_wait(barrier, 8 + 3 + 7 + 1 - home.astype(jnp.int32) + jnp.where(ends, 0, 1) + NZ - 1 - z)
 
     IN1, RT, RS, ACT = 0, 8, 16, 28
     YS, YC, ZR, RET, LG, WG, WD = 44, 46, 48, 49, 57, 65, 69
+    TAIL, ROW, ZALL, ENTRY = 72, 73, 77, 93
 
     for e, off in zip(groups, order):
         mail.post(pack.at[e], in1.at[z // 2], IN1 + z // 2, at(2 * e + c, y, x, half),
                   home if off == 0 else None)
+    mail.post(x_in.at[pl.ds(tokens - 16, 16)], tail, TAIL, (seq + jnp.where(ends, 0, 1), exp), ends)
     own_group = z // 2
     stay = pltpu.make_async_copy(pack.at[own_group], in1.at[own_group], local.at[NX + 1])
     pl.when(home)(stay.start)
@@ -140,6 +165,35 @@
     mail.post(wd_in, wd.at[c], WD, mate)
     for j in range(1, 8):
         mail.post(lgs, lgr.at[exp], LG + exp, (seq, lax.rem(exp + j, 8)))
+    mail.take(tail, TAIL, starts)
+    before_rows = tail[...].astype(F32)[8:16]
+    padded[0:8] = jnp.where(starts, 0.0, before_rows)
+    padded[8:8 + tokens] = x_in[...].astype(F32)
+    taps = conv_weight.shape[0]
+    convolved = conv_bias[...]
+    for k in range(taps):
+        convolved = convolved + conv_weight[k:k + 1, :] * padded[9 - taps + k:9 - taps + k + tokens]
+    activated = jax.nn.silu(convolved)
+    active[...] = activated
+    tiled(drive, step * activated)
+    states = rates.shape[0]
+
+    def own_step(t, carry):
+        d, u = delta[t], drive[t]
+        values = []
+        for n in range(states):
+            f = jnp.exp(d * rates[n])
+            factor[t, n] = f
+            values.append(f * carry[n] + b_and_c[0, n, t] * u)
+        return tuple(values) + (carry[states] + d,)
+
+    blank = jnp.zeros((tiles, 128), F32)
+    final_state = lax.fori_loop(0, tokens, own_step, (blank,) * (states + 1))
+    for n in range(states + 1):
+        rowend[y, n] = final_state[n]
+    for i, to_y in enumerate((near[1], near[-1], yfar)):
+        mail.post(rowend.at[y], rowend.at[y], ROW + y, at(z, to_y, x, c))
+
     pl.when(home)(stay.wait)
     for e, off in zip(groups, order):
         mail.take(in1.at[e], IN1 + e, home if off == 0 else None)
@@ -152,6 +206,71 @@
     mail.take(rt.at[0, other], RT + other)
     mail.post(rt.at[0, other], rt.at[2, other], RT + 4 + other, ypeer[1])
     mail.post(rt.at[0, other], rt.at[1, other], RT + 2 + other, ypeer[-1])
+    quarter = states // NY
+    for to_y in (near[1], near[-1], yfar):
+        mail.take(rowend.at[to_y], ROW + to_y)
+    ahead_sum, row_sum = blank, blank
+    for other_y in range(NY):
+        ahead_sum = jnp.where(y == other_y, row_sum, ahead_sum)
+        row_sum = row_sum + rowend[other_y, states]
+    for n in range(states):
+        total, mine_before = blank, blank
+        for other_y in range(NY):
+            mine_before = jnp.where(y == other_y, total, mine_before)
+            total = jnp.exp(rates[n] * rowend[other_y, states]) * total + rowend[other_y, n]
+        state[n] = mine_before
+        rowall[n // quarter, n % quarter] = total
+    for i in range(NY):
+        rowall[i, quarter] = row_sum
+    for later in range(1, NZ):
+        gone = z + later >= NZ
+        mail.post(rowall.at[y], zall.at[z], ZALL + z, at(jnp.where(gone, z, z + later), y, x, c), gone)
+
+    def along_z():
+        def fold(other_z, carry):
+            mail.take(zall.at[other_z], ZALL + other_z)
+            decay = zall[other_z, quarter]
+            return tuple(jnp.exp(rates[quarter * y + i] * decay) * carry[i] + zall[other_z, i]
+                         for i in range(quarter))
+
+        entering = lax.fori_loop(0, z, fold, (blank,) * quarter)
+        for i in range(quarter):
+            entry[y, i] = entering[i]
+        for to_y in (near[1], near[-1], yfar):
+            mail.post(entry.at[y], entry.at[y], ENTRY + y, at(z, to_y, x, c))
+
+    def enter():
+        for to_y in (near[1], near[-1], yfar):
+            mail.take(entry.at[to_y], ENTRY + to_y)
+        for n in range(states):
+            state[n] = state[n] + jnp.exp(rates[n] * ahead_sum) * entry[n // quarter, n % quarter]
+
+    pieces = 4
+
+    def scan_piece(piece):
+        def full_step(t, carry):
+            u = drive[t]
+            values, seen = [], None
+            for n in range(states):
+                value = factor[t, n] * carry[n] + b_and_c[0, n, t] * u
+                values.append(value)
+                term = b_and_c[1, n, t] * value
+                seen = term if seen is None else seen + term
+            reads[t] = seen
+            return tuple(values)
+
+        length = tokens // pieces
+        done = lax.fori_loop(piece * length, (piece + 1) * length, full_step,
+                             tuple(state[n] for n in range(states)))
+        for n in range(states):
+            state[n] = done[n]
+
+    def finish_mixer():
+        for j in range(tiles):
+            cols = slice(j * 128, (j + 1) * 128)
+            gate = jax.nn.silu(z_gate[:, cols].astype(F32))
+            mixed[:, cols] = ((reads[:, j, :] + d_skip[:, cols] * active[:, cols]) * gate).astype(BF)
+
     for copy in loads:
         copy.wait()
     for q in range(NX):
@@ -214,9 +333,10 @@
                 total += dot(act[k, q], wd[f, q * ff:(q + 1) * ff])
             prod[k, f] = total.astype(BF)
 
-    steps = [("g", 0), ("a", 0), ("g", 1), ("g", 2), ("a", 1), ("b", 0), ("a", 2), ("b", 1), ("c", 0), ("g", 3),
-             ("a", 3), ("b", 2), ("c", 1), ("d", 0), ("b", 3), ("c", 2), ("d", 1), ("w", 0), ("e", 0), ("c", 3),
-             ("d", 2), ("e", 1), ("d", 3), ("e", 2), ("e", 3)]
+    steps = [("g", 0), ("a", 0), ("g", 1), ("g", 2), ("a", 1), ("b", 0), ("z", 0), ("a", 2), ("b", 1), ("c", 0),
+             ("g", 3), ("a", 3), ("b", 2), ("c", 1), ("d", 0), ("y", 0), ("b", 3), ("c", 2), ("m", 0), ("d", 1),
+             ("w", 0), ("e", 0), ("m", 1), ("c", 3), ("d", 2), ("e", 1), ("m", 2), ("d", 3), ("e", 2), ("m", 3),
+             ("e", 3)]
     for what, k in steps:
         if what == "g":
             gathered(k)
@@ -228,6 +348,12 @@
             third(k)
         elif what == "d":
             fourth(k)
+        elif what == "z":
+            along_z()
+        elif what == "y":
+            enter()
+        elif what == "m":
+            scan_piece(k)
         elif what == "w":
             mail.take(wd.at[1 - c], WD)
         else:
@@ -264,6 +390,7 @@
     last = pltpu.make_async_copy(back.at[own_group], ret.at[own_group], local.at[NX + 2])
     pl.when(home)(last.start)
 
+    finish_mixer()
     for j in range(1, 8):
         q = lax.rem(exp + j, 8)
         mail.take(lgr.at[q], LG + q)
@@ -288,16 +415,24 @@
     mail.finish()
 
 
-def experts_of(hidden, router, expert_ids, w_gate, w_down):
+def local(x_in, z_gate, dt_low, dt_weight, dt_bias, a_log, conv_weight, conv_bias, d_skip, b_and_c,
+          hidden, router, expert_ids, w_gate, w_down):
     tokens, feats = hidden.shape
+    channels, states = x_in.shape[1], a_log.shape[0]
+    tiles, quarter = channels // 128, states // NY
     rows, ff = CAP * 8, w_gate.shape[1] // NX
     vm = pl.BlockSpec(memory_space=pltpu.VMEM)
     hbm = pl.BlockSpec(memory_space=pl.ANY)
+    sm = pl.BlockSpec(memory_space=pltpu.SMEM)
+
+    def row(a):
+        return a.reshape(1, channels)
+
     return pl.pallas_call(
-        expert_kernel,
-        out_shape=jax.ShapeDtypeStruct((tokens, feats), BF),
-        in_specs=[vm, vm, vm, hbm, hbm],
-        out_specs=vm,
+        layer_kernel,
+        out_shape=(jax.ShapeDtypeStruct((tokens, channels), BF), jax.ShapeDtypeStruct((tokens, feats), BF)),
+        in_specs=[vm] * 9 + [sm] + [vm] * 3 + [hbm] * 2,
+        out_specs=(vm, vm),
         scratch_shapes=[
             pltpu.VMEM((2, NX, feats, ff), BF),
             pltpu.VMEM((2, NX * ff, feats), BF),
@@ -316,121 +451,28 @@
             pltpu.VMEM((8, PAD, feats), BF),
             pltpu.VMEM((8, 128), F32),
             pltpu.VMEM((8, 8, 128), F32),
-            pltpu.SemaphoreType.DMA((96,)),
-            pltpu.SemaphoreType.DMA((96,)),
+            pltpu.VMEM((16, channels), BF),
+            pltpu.VMEM((8 + tokens, channels), F32),
+            pltpu.VMEM((tokens, channels), F32),
+            pltpu.VMEM((tokens, tiles, 128), F32),
+            pltpu.VMEM((tokens, tiles, 128), F32),
+            pltpu.VMEM((states, tiles, 128), F32),
+            pltpu.VMEM((tokens, states, tiles, 128), F32),
+            pltpu.VMEM((states, tiles, 128), F32),
+            pltpu.VMEM((NY, states + 1, tiles, 128), F32),
+            pltpu.VMEM((NY, quarter + 1, tiles, 128), F32),
+            pltpu.VMEM((NZ, quarter + 1, tiles, 128), F32),
+            pltpu.VMEM((NY, quarter, tiles, 128), F32),
+            pltpu.VMEM((tokens, tiles, 128), F32),
+            pltpu.SemaphoreType.DMA((128,)),
+            pltpu.SemaphoreType.DMA((128,)),
             pltpu.SemaphoreType.DMA((8,)),
         ],
         compiler_params=pltpu.CompilerParams(collective_id=0, has_side_effects=True,
                                              vmem_limit_bytes=60 * 1024 * 1024),
-        name="experts",
-    )(hidden, router.T, expert_ids.T, w_gate, w_down)
-
-
-def passed_along(value, axis, steps):
-    count = lax.axis_size(axis)
-    first, last = (max(0, -steps), min(count, count - steps))
-    return lax.ppermute(value, axis, [(source, source + steps) for source in range(first, last)])
-
-
-def carried_in(array, axis, join, neutral):
-    place = lax.axis_index(axis)
-    gathered = jax.tree.map(
-        lambda a, kind: lax.all_gather(a.astype(kind), axis), array, (jnp.bfloat16, jnp.bfloat16)
-    )
-    state = jax.tree.map(lambda a, e: jnp.zeros_like(a) + jnp.asarray(e, a.dtype), array, neutral)
-
-    def one(lap, state):
-        return join(
-            state,
-            jax.tree.map(
-                lambda a, own: lax.dynamic_index_in_dim(a, lap, 0, False).astype(own.dtype),
-                gathered,
-                array,
-            ),
-        )
-
-    return lax.fori_loop(0, place, one, state)
-
-
-def link_pairs(earlier, later):
-    return (earlier[0] * later[0], later[0] * earlier[1] + later[1])
-
-
-def mixer_scan(delta, activated, b_rows, c_rows, rates, start_state):
-    token_count, channels = delta.shape
-    block_len = 16
-    block_count = token_count // block_len
-
-    def regroup(values):
-        return values.reshape((block_count, block_len) + values.shape[1:])
-
-    def advance(carry, inputs):
-        running, product = carry
-        step_delta, step_x, step_b, step_c = inputs
-        reads = []
-        for position in range(block_len):
-            factor = jnp.exp(step_delta[position][None, :] * rates)
-            running = (
-                factor * running
-                + step_b[position][:, None] * (step_delta[position] * step_x[position])[None, :]
-            )
-            product = factor * product
-            reads.append(jnp.sum(step_c[position][:, None] * running, axis=0))
-        return ((running, product), (jnp.stack(reads),))
-
-    initial = (start_state, jnp.ones(rates.shape, jnp.float32))
-    finals, outputs = lax.scan(
-        advance, initial, (regroup(delta), regroup(activated), regroup(b_rows), regroup(c_rows))
-    )
-    readout = outputs[0].reshape(token_count, channels)
-    weighted_all = None
-    return (readout, weighted_all, finals[0], finals[1])
-
-
-def local(
-    x_in,
-    z_gate,
-    dt_low,
-    dt_weight,
-    dt_bias,
-    a_log,
-    conv_weight,
-    conv_bias,
-    d_skip,
-    b_and_c,
-    hidden,
-    router,
-    expert_ids,
-    w_gate,
-    w_down,
-):
-    tok_rows = x_in.shape[0]
-    kernel_taps = conv_weight.shape[0]
-    edge_rows = passed_along(x_in[tok_rows - (kernel_taps - 1) :], "seq", 1)
-    padded = jnp.concatenate([edge_rows, x_in], axis=0).astype(jnp.float32)
-    convolved = jnp.zeros(x_in.shape, jnp.float32) + conv_bias[None, :]
-    for offset in range(kernel_taps):
-        convolved = convolved + conv_weight[offset][None, :] * padded[offset : offset + tok_rows]
-    activated = jax.nn.silu(convolved)
-    delta = jax.nn.softplus(
-        jnp.dot(dt_low, dt_weight, preferred_element_type=jnp.float32) + dt_bias[None, :]
-    )
-    rates = -jnp.exp(a_log)
-    b_rows = b_and_c[0].T
-    c_rows = b_and_c[1].T
-    zero_state = jnp.zeros(rates.shape, jnp.float32)
-    readout, weighted_all, end_state, end_product = mixer_scan(
-        delta, activated, b_rows, c_rows, rates, zero_state
-    )
-    identity = (jnp.ones(rates.shape, jnp.float32), jnp.zeros(rates.shape, jnp.float32))
-    carried = carried_in((end_product, end_state), "seq", link_pairs, identity)
-    entering = carried[1]
-    readout = mixer_scan(delta, activated, b_rows, c_rows, rates, entering)[0]
-    mamba_out = (
-        (readout + d_skip[None, :] * activated) * jax.nn.silu(z_gate.astype(jnp.float32))
-    ).astype(jnp.bfloat16)
-    moe_out = experts_of(hidden, router, expert_ids, w_gate, w_down)
-    return (mamba_out, moe_out)
+        name="layer",
+    )(x_in, z_gate, dt_low, dt_weight, row(dt_bias), a_log, conv_weight, row(conv_bias), row(d_skip), b_and_c,
+      hidden, router.T, expert_ids.T, w_gate, w_down)
 
 
 def solution(mesh):

time: 371 us -> 119 us (0.32)
  the two profiles are of different devices: /device:TPU:504 before, /device:TPU:1 now
where the time goes in v2:
time: 119 us
  Pallas kernels  116 us (97%)
  local copies, waits for them, and re-layouts  3.04 us (3%)
    pallas_call x1, Pallas kernels, local(): pl.pallas_call(layer_kernel, out_shape=(jax.ShapeDtypeStruct((tokens, cha...  116 us
    unnamed x2, local copies, waits for them, and re-layouts  3.04 us

profile of v2, /device:TPU:1, one launch (start us, length us, event | category | flops | bytes accessed | tf_op | source)
XLA Modules:
  0.0 119.3 jit_solution(12277771801536429307)
XLA Ops:
  0.6 115.6 %layer.1 = (bf16[64,1024]{1,0:T(8,128)(2,1)}, bf16[64,512]{1,0:T(8,128)(2,1)}) custom-call(bf16[64,1024]{1,0:T(8,128)(2,1)} %x_in.1, bf16[64,1024]{1,0:T(8,128)(2,1)} %z_gate.1, bf16[64,256]{1,0:T(8,128)(2,1)} %dt_low.1, bf16[256,1024]{1,0:T(8,128)(2,1)} %dt_weight.1, f32[1,1024]{1,0:T(1,128)} %bitcast.6, f32[16,1024]{1,0:T(8,128)} %a_log.1, ...), custom_call_target="tpu_custom_call" | custom-call | tf_op jit(solution)/shard_map/layer/pallas_call | solution.py:431
  116.2 1.6 %copy.19 = bf16[64,1024]{1,0:T(8,128)(2,1)} copy(bf16[64,1024]{1,0:T(8,128)(2,1)} %get-tuple-element.4) | data formatting | bytes 262144
  117.8 1.5 %copy.20 = bf16[64,512]{1,0:T(8,128)(2,1)} copy(bf16[64,512]{1,0:T(8,128)(2,1)} %get-tuple-element.5) | data formatting | bytes 131072

commit v3 on v2

--- a/solution.py
+++ b/solution.py
@@ -8,11 +8,11 @@
 from jax.sharding import PartitionSpec as P
 
 CAP = 18
-PAD = 32
+PAD = 24
 NZ, NY, NX = 16, 4, 4
 MESH = pl.DeviceIdType.MESH
 BF, F32 = jnp.bfloat16, jnp.float32
-BATCHES = 4
+BATCHES = ((0, 0, 80), (1, 0, 144), (3, 0, 144), (2, 0, 144), (0, 80, 64))
 
 
 def dot(a, b):
@@ -81,12 +81,27 @@
 
     order = [4, 3, 5, 2, 6, 1, 7, 0]
     groups = [lax.rem(z // 2 + off, experts) for off in order]
-    for e, off in zip(groups, order):
-        to = at(2 * e + c, y, x, half)
+    away = jnp.logical_not(home)
+
+    def unless(cond, work):
+        pl.when(jnp.logical_not(cond))(work)
+
+    homes = [at(2 * e + half, y, x, half) for e in groups]
+    for to, off in zip(homes, order):
         if off == 0:
-            pl.when(jnp.logical_not(home))(functools.partial(greet, to))
+            unless(home, functools.partial(greet, to))
         else:
             greet(to)
+    feeds = [(f, e, off, at(2 * e + c, y, x, f)) for off, e in zip(order, groups) for f in range(2)]
+
+    def greet_feeds():
+        for f, e, off, to in feeds:
+            if off == 0:
+                unless(c == f, functools.partial(greet, to))
+            else:
+                greet(to)
+
+    pl.when(home)(greet_feeds)
     for to in (zpeer, ypeer[1], ypeer[-1]):
         greet(to)
     for j in range(1, 8):
@@ -147,18 +162,17 @@
     tiled(rates, -jnp.exp(a_log[...]))
 
     mail = Mail(send, recv)
-    pl.semaphore_wait(barrier, 8 + 3 + 7 + 1 - home.astype(jnp.int32) + jnp.where(ends, 0, 1) + NZ - 1 - z)
-
-    IN1, RT, RS, ACT = 0, 8, 16, 28
-    YS, YC, ZR, RET, LG, WG, WD = 44, 46, 48, 49, 57, 65, 69
-    TAIL, ROW, ZALL, ENTRY = 72, 73, 77, 93
-
-    for e, off in zip(groups, order):
-        mail.post(pack.at[e], in1.at[z // 2], IN1 + z // 2, at(2 * e + c, y, x, half),
-                  home if off == 0 else None)
+    pl.semaphore_wait(barrier, 8 + 3 + 7 + 1 + 14 * home.astype(jnp.int32) + jnp.where(ends, 0, 1) + NZ - 1 - z)
+
+    IN1, RT, RS, ACT = 0, 16, 24, 39
+    YS, YC, ZR, RET, LG, WG, WD = 59, 61, 65, 67, 75, 83, 87
+    TAIL, ROW, ZALL, ENTRY = 88, 89, 93, 109
+
+    for e, off, to in zip(groups, order, homes):
+        mail.post(pack.at[e], in1.at[c, z // 2], IN1 + 8 * c + z // 2, to, home if off == 0 else None)
     mail.post(x_in.at[pl.ds(tokens - 16, 16)], tail, TAIL, (seq + jnp.where(ends, 0, 1), exp), ends)
     own_group = z // 2
-    stay = pltpu.make_async_copy(pack.at[own_group], in1.at[own_group], local.at[NX + 1])
+    stay = pltpu.make_async_copy(pack.at[own_group], in1.at[c, own_group], local.at[NX + 1])
     pl.when(home)(stay.start)
     for q in range(NX):
         mail.post(wg_in.at[:, pl.ds(q * ff, ff)], wg.at[c, q], WG + q, mate)
@@ -195,17 +209,20 @@
         mail.post(rowend.at[y], rowend.at[y], ROW + y, at(z, to_y, x, c))
 
     pl.when(home)(stay.wait)
-    for e, off in zip(groups, order):
-        mail.take(in1.at[e], IN1 + e, home if off == 0 else None)
-
-    rt[0, half] = dot(tight, in1[...].reshape(experts * PAD, -1)).astype(BF)
-    other = 1 - half
-    mail.post(rt.at[0, half], rt.at[0, half], RT + half, zpeer)
-    mail.post(rt.at[0, half], rt.at[2, half], RT + 4 + half, ypeer[1])
-    mail.post(rt.at[0, half], rt.at[1, half], RT + 2 + half, ypeer[-1])
-    mail.take(rt.at[0, other], RT + other)
-    mail.post(rt.at[0, other], rt.at[2, other], RT + 4 + other, ypeer[1])
-    mail.post(rt.at[0, other], rt.at[1, other], RT + 2 + other, ypeer[-1])
+    for f, e, off, to in feeds:
+        mail.take(in1.at[f, e], IN1 + 8 * f + e, (away | (c == f)) if off == 0 else away)
+
+    def compact():
+        for f in range(2):
+            rt[0, f] = dot(tight, in1[f].reshape(experts * PAD, -1)).astype(BF)
+
+    pl.when(home)(compact)
+    for f in range(2):
+        mail.post(rt.at[0, f], rt.at[0, f], RT + f, zpeer, away)
+    for f in range(2):
+        mail.take(rt.at[0, f], RT + f, home)
+        mail.post(rt.at[0, f], rt.at[2, f], RT + 4 + f, ypeer[1])
+        mail.post(rt.at[0, f], rt.at[1, f], RT + 2 + f, ypeer[-1])
     quarter = states // NY
     for to_y in (near[1], near[-1], yfar):
         mail.take(rowend.at[to_y], ROW + to_y)
@@ -285,111 +302,116 @@
             mail.take(rt.at[2, 0], RT + 4)
             mail.post(rt.at[2, 0], rt.at[3, 0], RT + 6, ypeer[1])
             mail.take(rt.at[2, 1], RT + 5)
-        elif k == 3:
+        else:
             mail.take(rt.at[3, 0], RT + 6)
             mail.take(rt.at[3, 1], RT + 7)
 
-    def part(k, q):
-        return dot(rt[k, 0], wg[0, q]) + dot(rt[k, 1], wg[1, q])
-
-    way = [1 if k % 2 == 0 else -1 for k in range(BATCHES)]
-    kept = {}
-
-    def first(k):
-        d = way[k]
-        sbuf[k, 0] = part(k, xs[2]).astype(BF)
-        mail.post(sbuf.at[k, 0], rbuf.at[k, 0], RS + 3 * k, xpeer[d])
-        sbuf[k, 1] = part(k, xs[-d]).astype(BF)
-        mail.post(sbuf.at[k, 1], rbuf.at[k, 1], RS + 3 * k + 1, xpeer[-d])
-        sbuf[k, 2] = part(k, xs[d]).astype(BF)
-        sbuf[k, 3] = part(k, x).astype(BF)
-
-    def second(k):
-        d = way[k]
-        mail.take(rbuf.at[k, 0], RS + 3 * k)
-        sbuf[k, 4] = (sbuf[k, 2].astype(F32) + rbuf[k, 0].astype(F32)).astype(BF)
-        mail.post(sbuf.at[k, 4], rbuf.at[k, 2], RS + 3 * k + 2, xpeer[d])
-
-    def third(k):
-        mail.take(rbuf.at[k, 1], RS + 3 * k + 1)
-        mail.take(rbuf.at[k, 2], RS + 3 * k + 2)
-        total = sbuf[k, 3].astype(F32) + rbuf[k, 1].astype(F32) + rbuf[k, 2].astype(F32)
-        act[k, x] = jax.nn.silu(total).astype(BF)
+    def span(b):
+        return pl.ds(0, BATCHES[b][2])
+
+    def part(b, q):
+        k, start, count = BATCHES[b]
+        held = pl.ds(start, count)
+        return dot(rt[k, 0, held], wg[0, q]) + dot(rt[k, 1, held], wg[1, q])
+
+    way = [1, -1, 1, -1, 1]
+
+    def first(b):
+        d, r = way[b], span(b)
+        sbuf[b, 0, r] = part(b, xs[2]).astype(BF)
+        mail.post(sbuf.at[b, 0, r], rbuf.at[b, 0, r], RS + 3 * b, xpeer[d])
+        sbuf[b, 1, r] = part(b, xs[-d]).astype(BF)
+        mail.post(sbuf.at[b, 1, r], rbuf.at[b, 1, r], RS + 3 * b + 1, xpeer[-d])
+        sbuf[b, 2, r] = part(b, xs[d]).astype(BF)
+        sbuf[b, 3, r] = part(b, x).astype(BF)
+
+    def second(b):
+        d, r = way[b], span(b)
+        mail.take(rbuf.at[b, 0, r], RS + 3 * b)
+        sbuf[b, 4, r] = (sbuf[b, 2, r].astype(F32) + rbuf[b, 0, r].astype(F32)).astype(BF)
+        mail.post(sbuf.at[b, 4, r], rbuf.at[b, 2, r], RS + 3 * b + 2, xpeer[d])
+
+    def third(b):
+        r = span(b)
+        mail.take(rbuf.at[b, 1, r], RS + 3 * b + 1)
+        mail.take(rbuf.at[b, 2, r], RS + 3 * b + 2)
+        total = sbuf[b, 3, r].astype(F32) + rbuf[b, 1, r].astype(F32) + rbuf[b, 2, r].astype(F32)
+        act[b, x, r] = jax.nn.silu(total).astype(BF)
         for d in (1, -1):
-            mail.post(act.at[k, x], act.at[k, x], ACT + 4 * k + x, xpeer[d])
-
-    def fourth(k):
-        d = way[k]
-        mail.take(act.at[k, xs[-d]], ACT + 4 * k + xs[-d])
-        mail.post(act.at[k, xs[-d]], act.at[k, xs[-d]], ACT + 4 * k + xs[-d], xpeer[d])
-
-    def down(k):
-        d = way[k]
-        mail.take(act.at[k, xs[d]], ACT + 4 * k + xs[d])
-        mail.take(act.at[k, xs[2]], ACT + 4 * k + xs[2])
+            mail.post(act.at[b, x, r], act.at[b, x, r], ACT + 4 * b + x, xpeer[d])
+
+    def fourth(b):
+        d, r = way[b], span(b)
+        mail.take(act.at[b, xs[-d], r], ACT + 4 * b + xs[-d])
+        mail.post(act.at[b, xs[-d], r], act.at[b, xs[-d], r], ACT + 4 * b + xs[-d], xpeer[d])
+
+    def down(b):
+        d, r = way[b], span(b)
+        k, start, count = BATCHES[b]
+        mail.take(act.at[b, xs[d], r], ACT + 4 * b + xs[d])
+        mail.take(act.at[b, xs[2], r], ACT + 4 * b + xs[2])
         for f in range(2):
-            total = dot(act[k, 0], wd[f, 0:ff])
+            total = dot(act[b, 0, r], wd[f, 0:ff])
             for q in range(1, NX):
-                total += dot(act[k, q], wd[f, q * ff:(q + 1) * ff])
-            prod[k, f] = total.astype(BF)
-
-    steps = [("g", 0), ("a", 0), ("g", 1), ("g", 2), ("a", 1), ("b", 0), ("z", 0), ("a", 2), ("b", 1), ("c", 0),
-             ("g", 3), ("a", 3), ("b", 2), ("c", 1), ("d", 0), ("y", 0), ("b", 3), ("c", 2), ("m", 0), ("d", 1),
-             ("w", 0), ("e", 0), ("m", 1), ("c", 3), ("d", 2), ("e", 1), ("m", 2), ("d", 3), ("e", 2), ("m", 3),
-             ("e", 3)]
-    for what, k in steps:
-        if what == "g":
-            gathered(k)
-        elif what == "a":
-            first(k)
-        elif what == "b":
-            second(k)
-        elif what == "c":
-            third(k)
-        elif what == "d":
-            fourth(k)
-        elif what == "z":
-            along_z()
-        elif what == "y":
-            enter()
-        elif what == "m":
-            scan_piece(k)
-        elif what == "w":
-            mail.take(wd.at[1 - c], WD)
-        else:
-            down(k)
-
-    mail.post(prod.at[3, 0], yc.at[0], YC, ypeer[1])
-    mail.post(prod.at[3, 1], yc.at[1], YC + 1, ypeer[-1])
-    mail.post(prod.at[1, 1], ys.at[1], YS + 1, ypeer[1])
-    mail.post(prod.at[2, 0], ys.at[0], YS, ypeer[-1])
-    mail.take(yc.at[0], YC)
-    zs[0] = (prod[1, 0].astype(F32) + yc[0].astype(F32)).astype(BF)
-    mail.post(zs.at[0], yc.at[2], RET + 21, ypeer[1])
-    mail.take(yc.at[1], YC + 1)
-    zs[1] = (prod[2, 1].astype(F32) + yc[1].astype(F32)).astype(BF)
-    mail.post(zs.at[1], yc.at[3], RET + 22, ypeer[-1])
+                total += dot(act[b, q, r], wd[f, q * ff:(q + 1) * ff])
+            prod[k, f, pl.ds(start, count)] = total.astype(BF)
+
+    def home_far():
+        mail.post(prod.at[3, 0], yc.at[0], YC, ypeer[1])
+        mail.post(prod.at[3, 1], yc.at[1], YC + 1, ypeer[-1])
+
+    def home_next():
+        mail.take(yc.at[0], YC)
+        zs[0] = (prod[1, 0].astype(F32) + yc[0].astype(F32)).astype(BF)
+        mail.post(zs.at[0], yc.at[2], YC + 2, ypeer[1])
+
+    def home_previous():
+        mail.post(prod.at[2, 0], ys.at[0], YS, ypeer[-1])
+        mail.take(yc.at[1], YC + 1)
+        zs[1] = (prod[2, 1].astype(F32) + yc[1].astype(F32)).astype(BF)
+        mail.post(zs.at[1], yc.at[3], YC + 3, ypeer[-1])
+
+    steps = [
+        ("first", 0), ("block", 1), ("first", 1), ("second", 0), ("block", 2), ("block", 3), ("first", 2), ("second", 1),
+        ("third", 0), ("first", 3), ("second", 2), ("third", 1), ("fourth", 0), ("first", 4), ("second", 3), ("third", 2),
+        ("fourth", 1), ("weights", 0), ("down", 0), ("second", 4), ("third", 3), ("fourth", 2), ("down", 1), ("single", 0),
+        ("third", 4), ("fourth", 3), ("down", 2), ("far", 0), ("scan", 0), ("fourth", 4), ("next", 0), ("down", 3),
+        ("previous", 0), ("down", 4)]
+    does = {"first": first, "second": second, "third": third, "fourth": fourth, "down": down, "block": gathered,
+            "far": lambda b: home_far(), "next": lambda b: home_next(), "previous": lambda b: home_previous(),
+            "single": lambda b: mail.post(prod.at[1, 1], ys.at[1], YS + 1, ypeer[1]),
+            "scan": lambda b: along_z(), "weights": lambda b: mail.take(wd.at[1 - c], WD)}
+    for what, b in steps:
+        does[what](b)
     mail.take(ys.at[0], YS)
     mail.take(ys.at[1], YS + 1)
-    mail.take(yc.at[2], RET + 21)
-    mail.take(yc.at[3], RET + 22)
+    mail.take(yc.at[2], YC + 2)
+    mail.take(yc.at[3], YC + 3)
 
     def over_y(f):
         return prod[0, f].astype(F32) + ys[f].astype(F32) + yc[2 + f].astype(F32)
 
-    zs[2] = over_y(other).astype(BF)
-    mail.post(zs.at[2], zr, ZR, zpeer)
-    mine = over_y(half)
-    mail.take(zr, ZR)
-    final = (mine + zr[...].astype(F32)).astype(BF)
-    back[...] = dot(loose, final).astype(BF).reshape(back.shape)
-
-    for i, off in zip(groups, order):
-        mail.post(back.at[i], ret.at[own_group], RET + own_group, at(2 * i + c, y, x, half),
-                  home if off == 0 else None)
-    last = pltpu.make_async_copy(back.at[own_group], ret.at[own_group], local.at[NX + 2])
+    for f in range(2):
+        total = over_y(f)
+        zs[2 + f] = total.astype(BF)
+        mail.post(zs.at[2 + f], zr.at[f], ZR + f, zpeer, home)
+    for f in range(2):
+        mail.take(zr.at[f], ZR + f, away)
+
+    def spread():
+        for f in range(2):
+            whole = (over_y(f) + zr[f].astype(F32)).astype(BF)
+            back[f] = dot(loose, whole).astype(BF).reshape(back.shape[1:])
+
+    pl.when(home)(spread)
+    for f, e, off, to in feeds:
+        mail.post(back.at[f, e], ret.at[own_group], RET + own_group, to, (away | (c == f)) if off == 0 else away)
+    last = pltpu.make_async_copy(back.at[c, own_group], ret.at[own_group], local.at[NX + 2])
     pl.when(home)(last.start)
 
+    enter()
+    for piece in range(pieces):
+        scan_piece(piece)
     finish_mixer()
     for j in range(1, 8):
         q = lax.rem(exp + j, 8)
@@ -437,17 +459,17 @@
             pltpu.VMEM((2, NX, feats, ff), BF),
             pltpu.VMEM((2, NX * ff, feats), BF),
             pltpu.VMEM((8, PAD, feats), BF),
-            pltpu.VMEM((8, PAD, feats), BF),
-            pltpu.VMEM((BATCHES, 2, rows, feats), BF),
-            pltpu.VMEM((BATCHES, 5, rows, ff), BF),
-            pltpu.VMEM((BATCHES, 3, rows, ff), BF),
-            pltpu.VMEM((BATCHES, NX, rows, ff), BF),
-            pltpu.VMEM((BATCHES, 2, rows, feats), BF),
+            pltpu.VMEM((2, 8, PAD, feats), BF),
+            pltpu.VMEM((4, 2, rows, feats), BF),
+            pltpu.VMEM((len(BATCHES), 5, rows, ff), BF),
+            pltpu.VMEM((len(BATCHES), 3, rows, ff), BF),
+            pltpu.VMEM((len(BATCHES), NX, rows, ff), BF),
+            pltpu.VMEM((4, 2, rows, feats), BF),
             pltpu.VMEM((2, rows, feats), BF),
             pltpu.VMEM((4, rows, feats), BF),
-            pltpu.VMEM((3, rows, feats), BF),
-            pltpu.VMEM((rows, feats), BF),
-            pltpu.VMEM((8, PAD, feats), BF),
+            pltpu.VMEM((4, rows, feats), BF),
+            pltpu.VMEM((2, rows, feats), BF),
+            pltpu.VMEM((2, 8, PAD, feats), BF),
             pltpu.VMEM((8, PAD, feats), BF),
             pltpu.VMEM((8, 128), F32),
             pltpu.VMEM((8, 8, 128), F32),

time: 119 us -> 113 us (0.950)
  Pallas kernels: 116 us -> 109 us
    pallas_call x1, Pallas kernels: 116 us -> 109 us  [local(): pl.pallas_call(layer_kernel, out_shape=(jax.ShapeDtypeStruct((tokens, cha...]
where the time goes in v3:
time: 113 us
  Pallas kernels  109 us (96%)
  local copies, waits for them, and re-layouts  3.04 us (3%)
    pallas_call x1, Pallas kernels, local(): pl.pallas_call(layer_kernel, out_shape=(jax.ShapeDtypeStruct((tokens, cha...  109 us
    unnamed x2, local copies, waits for them, and re-layouts  3.04 us

profile of v3, /device:TPU:1, one launch (start us, length us, event | category | flops | bytes accessed | tf_op | source)
XLA Modules:
  0.0 112.7 jit_solution(7797325132839150471)
XLA Ops:
  0.6 109.1 %layer.1 = (bf16[64,1024]{1,0:T(8,128)(2,1)}, bf16[64,512]{1,0:T(8,128)(2,1)}) custom-call(bf16[64,1024]{1,0:T(8,128)(2,1)} %x_in.1, bf16[64,1024]{1,0:T(8,128)(2,1)} %z_gate.1, bf16[64,256]{1,0:T(8,128)(2,1)} %dt_low.1, bf16[256,1024]{1,0:T(8,128)(2,1)} %dt_weight.1, f32[1,1024]{1,0:T(1,128)} %bitcast.6, f32[16,1024]{1,0:T(8,128)} %a_log.1, ...), custom_call_target="tpu_custom_call" | custom-call | tf_op jit(solution)/shard_map/layer/pallas_call | solution.py:453
  109.7 1.6 %copy.19 = bf16[64,1024]{1,0:T(8,128)(2,1)} copy(bf16[64,1024]{1,0:T(8,128)(2,1)} %get-tuple-element.4) | data formatting | bytes 262144
  111.3 1.5 %copy.20 = bf16[64,512]{1,0:T(8,128)(2,1)} copy(bf16[64,512]{1,0:T(8,128)(2,1)} %get-tuple-element.5) | data formatting | bytes 131072

commit v4 on v3

--- a/solution.py
+++ b/solution.py
@@ -12,7 +12,8 @@
 NZ, NY, NX = 16, 4, 4
 MESH = pl.DeviceIdType.MESH
 BF, F32 = jnp.bfloat16, jnp.float32
-BATCHES = ((0, 0, 80), (1, 0, 144), (3, 0, 144), (2, 0, 144), (0, 80, 64))
+SHARE = 4
+BATCHES = (((0, 0),), ((1, 0), (2, 0)), ((3, 0), (3, 1)), ((1, 1), (2, 1)), ((0, 1),))
 
 
 def dot(a, b):
@@ -53,7 +54,7 @@
 
 def layer_kernel(x_in, z_gate, dt_low, dt_weight, dt_bias, a_log, conv_weight, conv_bias, d_skip, b_and_c,
                  hid, router_t, ids_t, wg_in, wd_in, mixed, out,
-                 wg, wd, pack, in1, rt, sbuf, rbuf, act, prod, ys, yc, zs, zr, back, ret, lgs, lgr,
+                 wg, wd, pack, in1, rt, sbuf, rbuf, act, prod, ys, yc, zs, zr, back, ret, lgs, lgr, zb,
                  tail, padded, active, delta, drive, rates, factor, state, rowend, rowall, zall, entry, reads,
                  send, recv, local):
     seq, exp = lax.axis_index("seq"), lax.axis_index("exp")
@@ -74,34 +75,30 @@
     experts = 8
 
     barrier = pltpu.get_barrier_semaphore()
-    home = half == c
 
     def greet(to):
         pl.semaphore_signal(barrier, inc=1, device_id=to, device_id_type=MESH)
 
+    def unless(cond, work):
+        pl.when(jnp.logical_not(cond))(work)
+
     order = [4, 3, 5, 2, 6, 1, 7, 0]
     groups = [lax.rem(z // 2 + off, experts) for off in order]
-    away = jnp.logical_not(home)
-
-    def unless(cond, work):
-        pl.when(jnp.logical_not(cond))(work)
-
-    homes = [at(2 * e + half, y, x, half) for e in groups]
-    for to, off in zip(homes, order):
-        if off == 0:
-            unless(home, functools.partial(greet, to))
+    wide, turn_j = lax.rem(z // 2, 2), z // 4
+    mine = (half == c) & (wide == half)
+    targets = [(off == 0, e, at(2 * e + wide, y, x, half)) for off, e in zip(order, groups)]
+    feeds = [(f, j, at(4 * j + 2 * half + c, y, x, f)) for j in range(SHARE) for f in range(2)]
+
+    def is_me(f, j):
+        return mine & (c == f) & (turn_j == j)
+
+    for near_one, e, to in targets:
+        if near_one:
+            unless(mine, functools.partial(greet, to))
         else:
             greet(to)
-    feeds = [(f, e, off, at(2 * e + c, y, x, f)) for off, e in zip(order, groups) for f in range(2)]
-
-    def greet_feeds():
-        for f, e, off, to in feeds:
-            if off == 0:
-                unless(c == f, functools.partial(greet, to))
-            else:
-                greet(to)
-
-    pl.when(home)(greet_feeds)
+    for f, j, to in feeds:
+        unless(is_me(f, j), functools.partial(greet, to))
     for to in (zpeer, ypeer[1], ypeer[-1]):
         greet(to)
     for j in range(1, 8):
@@ -140,14 +137,14 @@
     pack[...] = dot(selector, h).astype(BF).reshape(pack.shape)
     lg = lax.dot_general(router_t[...], h, (((1,), (1,)), ((), ())), preferred_element_type=F32)
     lgs[...] = jnp.concatenate([lg, jnp.zeros((experts, 128 - tokens), F32)], axis=1)
-    rows = CAP * experts
-    r_c = lax.broadcasted_iota(jnp.int32, (rows, experts * PAD), 0)
-    q_c = lax.broadcasted_iota(jnp.int32, (rows, experts * PAD), 1)
-    group = sum((r_c >= CAP * m).astype(jnp.int32) for m in range(1, experts))
+    rows = CAP * SHARE
+    r_c = lax.broadcasted_iota(jnp.int32, (rows, SHARE * PAD), 0)
+    q_c = lax.broadcasted_iota(jnp.int32, (rows, SHARE * PAD), 1)
+    group = sum((r_c >= CAP * m).astype(jnp.int32) for m in range(1, SHARE))
     tight = jnp.where(q_c == r_c + (PAD - CAP) * group, 1.0, 0.0).astype(BF)
-    q_e = lax.broadcasted_iota(jnp.int32, (experts * PAD, rows), 0)
-    r_e = lax.broadcasted_iota(jnp.int32, (experts * PAD, rows), 1)
-    group_e = sum((r_e >= CAP * m).astype(jnp.int32) for m in range(1, experts))
+    q_e = lax.broadcasted_iota(jnp.int32, (SHARE * PAD, rows), 0)
+    r_e = lax.broadcasted_iota(jnp.int32, (SHARE * PAD, rows), 1)
+    group_e = sum((r_e >= CAP * m).astype(jnp.int32) for m in range(1, SHARE))
     loose = jnp.where(q_e == r_e + (PAD - CAP) * group_e, 1.0, 0.0).astype(BF)
 
     channels = x_in.shape[1]
@@ -162,18 +159,17 @@
     tiled(rates, -jnp.exp(a_log[...]))
 
     mail = Mail(send, recv)
-    pl.semaphore_wait(barrier, 8 + 3 + 7 + 1 + 14 * home.astype(jnp.int32) + jnp.where(ends, 0, 1) + NZ - 1 - z)
-
-    IN1, RT, RS, ACT = 0, 16, 24, 39
-    YS, YC, ZR, RET, LG, WG, WD = 59, 61, 65, 67, 75, 83, 87
-    TAIL, ROW, ZALL, ENTRY = 88, 89, 93, 109
-
-    for e, off, to in zip(groups, order, homes):
-        mail.post(pack.at[e], in1.at[c, z // 2], IN1 + 8 * c + z // 2, to, home if off == 0 else None)
+    pl.semaphore_wait(barrier, 16 + 3 + 7 + 1 - 2 * mine.astype(jnp.int32) + jnp.where(ends, 0, 1) + NZ - 1 - z)
+
+    IN1, RT, RS, ACT, YC, YS, ZR = 0, 8, 18, 33, 53, 57, 61
+    RET, LG, WG, WD, TAIL, ROW, ZALL, ENTRY = 62, 70, 78, 82, 83, 84, 88, 104
+
+    for near_one, e, to in targets:
+        mail.post(pack.at[e], in1.at[c, turn_j], IN1 + 4 * c + turn_j, to, mine if near_one else None)
     mail.post(x_in.at[pl.ds(tokens - 16, 16)], tail, TAIL, (seq + jnp.where(ends, 0, 1), exp), ends)
     own_group = z // 2
-    stay = pltpu.make_async_copy(pack.at[own_group], in1.at[c, own_group], local.at[NX + 1])
-    pl.when(home)(stay.start)
+    stay = pltpu.make_async_copy(pack.at[own_group], in1.at[c, turn_j], local.at[NX + 1])
+    pl.when(mine)(stay.start)
     for q in range(NX):
         mail.post(wg_in.at[:, pl.ds(q * ff, ff)], wg.at[c, q], WG + q, mate)
     mail.post(wd_in, wd.at[c], WD, mate)
@@ -208,21 +204,18 @@
     for i, to_y in enumerate((near[1], near[-1], yfar)):
         mail.post(rowend.at[y], rowend.at[y], ROW + y, at(z, to_y, x, c))
 
-    pl.when(home)(stay.wait)
-    for f, e, off, to in feeds:
-        mail.take(in1.at[f, e], IN1 + 8 * f + e, (away | (c == f)) if off == 0 else away)
-
-    def compact():
-        for f in range(2):
-            rt[0, f] = dot(tight, in1[f].reshape(experts * PAD, -1)).astype(BF)
-
-    pl.when(home)(compact)
+    pl.when(mine)(stay.wait)
+    for f, j, to in feeds:
+        mail.take(in1.at[f, j], IN1 + 4 * f + j, is_me(f, j))
+    feats = hid.shape[1]
+    cols = [pl.ds(f * feats, feats) for f in range(2)]
+    share = [half, 1 - half]
     for f in range(2):
-        mail.post(rt.at[0, f], rt.at[0, f], RT + f, zpeer, away)
-    for f in range(2):
-        mail.take(rt.at[0, f], RT + f, home)
-        mail.post(rt.at[0, f], rt.at[2, f], RT + 4 + f, ypeer[1])
-        mail.post(rt.at[0, f], rt.at[1, f], RT + 2 + f, ypeer[-1])
+        rt[0, half, :, cols[f]] = dot(tight, in1[f].reshape(SHARE * PAD, -1)).astype(BF)
+    for w in share[:1]:
+        mail.post(rt.at[0, w], rt.at[2, w], RT + 4 + w, ypeer[1])
+        mail.post(rt.at[0, w], rt.at[1, w], RT + 2 + w, ypeer[-1])
+        mail.post(rt.at[0, w], rt.at[0, w], RT + w, zpeer)
     quarter = states // NY
     for to_y in (near[1], near[-1], yfar):
         mail.take(rowend.at[to_y], ROW + to_y)
@@ -293,50 +286,62 @@
     for q in range(NX):
         mail.take(wg.at[1 - c, q], WG + q)
 
-    def gathered(k):
-        if k == 1:
-            mail.take(rt.at[1, 1], RT + 3)
-            mail.post(rt.at[1, 1], rt.at[3, 1], RT + 7, ypeer[-1])
-            mail.take(rt.at[1, 0], RT + 2)
-        elif k == 2:
-            mail.take(rt.at[2, 0], RT + 4)
-            mail.post(rt.at[2, 0], rt.at[3, 0], RT + 6, ypeer[1])
-            mail.take(rt.at[2, 1], RT + 5)
+    def gathered(k, i):
+        w = share[i]
+        if k == 0:
+            mail.take(rt.at[0, w], RT + w)
+            mail.post(rt.at[0, w], rt.at[2, w], RT + 4 + w, ypeer[1])
+            mail.post(rt.at[0, w], rt.at[1, w], RT + 2 + w, ypeer[-1])
+        elif k < 3:
+            mail.take(rt.at[k, w], RT + 2 * k + w)
+            f = k - 1 if k == 1 else 1
+            mail.post(rt.at[k, w, :, cols[f]], rt.at[3, w, :, cols[f]], RT + 6 + 2 * w + f, ypeer[-1 if k == 1 else 1])
         else:
-            mail.take(rt.at[3, 0], RT + 6)
-            mail.take(rt.at[3, 1], RT + 7)
+            for f in range(2):
+                mail.take(rt.at[3, w, :, cols[f]], RT + 6 + 2 * w + f)
+
+    def take_down():
+        mail.take(wd.at[1 - c], WD)
+
+    def part(b, i, q):
+        k, w = BATCHES[b][i]
+        held = rt.at[k, share[w]]
+        return dot(held[:, cols[0]], wg[0, q]) + dot(held[:, cols[1]], wg[1, q])
+
+    way = [1, -1, 1, -1, 1]
+
+    def blocks(b):
+        return range(len(BATCHES[b]))
 
     def span(b):
-        return pl.ds(0, BATCHES[b][2])
-
-    def part(b, q):
-        k, start, count = BATCHES[b]
-        held = pl.ds(start, count)
-        return dot(rt[k, 0, held], wg[0, q]) + dot(rt[k, 1, held], wg[1, q])
-
-    way = [1, -1, 1, -1, 1]
+        return pl.ds(0, len(BATCHES[b]))
 
     def first(b):
         d, r = way[b], span(b)
-        sbuf[b, 0, r] = part(b, xs[2]).astype(BF)
+        for i in blocks(b):
+            sbuf[b, 0, i] = part(b, i, xs[2]).astype(BF)
         mail.post(sbuf.at[b, 0, r], rbuf.at[b, 0, r], RS + 3 * b, xpeer[d])
-        sbuf[b, 1, r] = part(b, xs[-d]).astype(BF)
+        for i in blocks(b):
+            sbuf[b, 1, i] = part(b, i, xs[-d]).astype(BF)
         mail.post(sbuf.at[b, 1, r], rbuf.at[b, 1, r], RS + 3 * b + 1, xpeer[-d])
-        sbuf[b, 2, r] = part(b, xs[d]).astype(BF)
-        sbuf[b, 3, r] = part(b, x).astype(BF)
+        for i in blocks(b):
+            sbuf[b, 2, i] = part(b, i, xs[d]).astype(BF)
+            sbuf[b, 3, i] = part(b, i, x).astype(BF)
 
     def second(b):
         d, r = way[b], span(b)
         mail.take(rbuf.at[b, 0, r], RS + 3 * b)
-        sbuf[b, 4, r] = (sbuf[b, 2, r].astype(F32) + rbuf[b, 0, r].astype(F32)).astype(BF)
+        for i in blocks(b):
+            sbuf[b, 4, i] = (sbuf[b, 2, i].astype(F32) + rbuf[b, 0, i].astype(F32)).astype(BF)
         mail.post(sbuf.at[b, 4, r], rbuf.at[b, 2, r], RS + 3 * b + 2, xpeer[d])
 
     def third(b):
         r = span(b)
         mail.take(rbuf.at[b, 1, r], RS + 3 * b + 1)
         mail.take(rbuf.at[b, 2, r], RS + 3 * b + 2)
-        total = sbuf[b, 3, r].astype(F32) + rbuf[b, 1, r].astype(F32) + rbuf[b, 2, r].astype(F32)
-        act[b, x, r] = jax.nn.silu(total).astype(BF)
+        for i in blocks(b):
+            total = sbuf[b, 3, i].astype(F32) + rbuf[b, 1, i].astype(F32) + rbuf[b, 2, i].astype(F32)
+            act[b, x, i] = jax.nn.silu(total).astype(BF)
         for d in (1, -1):
             mail.post(act.at[b, x, r], act.at[b, x, r], ACT + 4 * b + x, xpeer[d])
 
@@ -347,67 +352,55 @@
 
     def down(b):
         d, r = way[b], span(b)
-        k, start, count = BATCHES[b]
         mail.take(act.at[b, xs[d], r], ACT + 4 * b + xs[d])
         mail.take(act.at[b, xs[2], r], ACT + 4 * b + xs[2])
+        for i in blocks(b):
+            k, w = BATCHES[b][i]
+            for f in range(2):
+                total = dot(act[b, 0, i], wd[f, 0:ff])
+                for q in range(1, NX):
+                    total += dot(act[b, q, i], wd[f, q * ff:(q + 1) * ff])
+                prod[k, share[w], :, cols[f]] = total.astype(BF)
+
+    def far(i):
+        w = share[i]
+        for f, d in ((0, 1), (1, -1)):
+            mail.post(prod.at[3, w, :, cols[f]], yc.at[w, f], YC + 2 * w + f, ypeer[d])
+
+    def combine(i):
+        w = share[i]
+        for f, d in ((0, 1), (1, -1)):
+            mail.take(yc.at[w, f], YC + 2 * w + f)
+            zs[w, f, :, cols[f]] = (prod[1 + f, w, :, cols[f]].astype(F32) + yc[w, f].astype(F32)).astype(BF)
+            zs[w, f, :, cols[1 - f]] = prod[1 + f, w, :, cols[1 - f]]
+            mail.post(zs.at[w, f], ys.at[w, f], YS + 2 * w + f, ypeer[d])
+
+    steps = [
+        (first, 0), (gathered, 1, 0), (gathered, 2, 0), (gathered, 0, 1), (first, 1), (second, 0), (gathered, 3, 0),
+        (third, 0), (second, 1), (gathered, 1, 1), (gathered, 2, 1), (fourth, 0), (gathered, 3, 1), (first, 2),
+        (third, 1), (first, 3), (second, 2), (fourth, 1), (take_down,), (down, 0), (first, 4), (second, 3), (third, 2),
+        (down, 1), (along_z,), (second, 4), (fourth, 2), (third, 3), (down, 2), (far, 0), (far, 1), (third, 4),
+        (fourth, 3), (combine, 0), (down, 3), (combine, 1), (fourth, 4), (down, 4)]
+    for step_of, *which in steps:
+        step_of(*which)
+
+    def over_y(i):
+        w = share[i]
         for f in range(2):
-            total = dot(act[b, 0, r], wd[f, 0:ff])
-            for q in range(1, NX):
-                total += dot(act[b, q, r], wd[f, q * ff:(q + 1) * ff])
-            prod[k, f, pl.ds(start, count)] = total.astype(BF)
-
-    def home_far():
-        mail.post(prod.at[3, 0], yc.at[0], YC, ypeer[1])
-        mail.post(prod.at[3, 1], yc.at[1], YC + 1, ypeer[-1])
-
-    def home_next():
-        mail.take(yc.at[0], YC)
-        zs[0] = (prod[1, 0].astype(F32) + yc[0].astype(F32)).astype(BF)
-        mail.post(zs.at[0], yc.at[2], YC + 2, ypeer[1])
-
-    def home_previous():
-        mail.post(prod.at[2, 0], ys.at[0], YS, ypeer[-1])
-        mail.take(yc.at[1], YC + 1)
-        zs[1] = (prod[2, 1].astype(F32) + yc[1].astype(F32)).astype(BF)
-        mail.post(zs.at[1], yc.at[3], YC + 3, ypeer[-1])
-
-    steps = [
-        ("first", 0), ("block", 1), ("first", 1), ("second", 0), ("block", 2), ("block", 3), ("first", 2), ("second", 1),
-        ("third", 0), ("first", 3), ("second", 2), ("third", 1), ("fourth", 0), ("first", 4), ("second", 3), ("third", 2),
-        ("fourth", 1), ("weights", 0), ("down", 0), ("second", 4), ("third", 3), ("fourth", 2), ("down", 1), ("single", 0),
-        ("third", 4), ("fourth", 3), ("down", 2), ("far", 0), ("scan", 0), ("fourth", 4), ("next", 0), ("down", 3),
-        ("previous", 0), ("down", 4)]
-    does = {"first": first, "second": second, "third": third, "fourth": fourth, "down": down, "block": gathered,
-            "far": lambda b: home_far(), "next": lambda b: home_next(), "previous": lambda b: home_previous(),
-            "single": lambda b: mail.post(prod.at[1, 1], ys.at[1], YS + 1, ypeer[1]),
-            "scan": lambda b: along_z(), "weights": lambda b: mail.take(wd.at[1 - c], WD)}
-    for what, b in steps:
-        does[what](b)
-    mail.take(ys.at[0], YS)
-    mail.take(ys.at[1], YS + 1)
-    mail.take(yc.at[2], YC + 2)
-    mail.take(yc.at[3], YC + 3)
-
-    def over_y(f):
-        return prod[0, f].astype(F32) + ys[f].astype(F32) + yc[2 + f].astype(F32)
-
+            mail.take(ys.at[w, f], YS + 2 * w + f)
+        return prod[0, w].astype(F32) + ys[w, 0].astype(F32) + ys[w, 1].astype(F32)
+
+    zb[...] = over_y(1).astype(BF)
+    mail.post(zb, zr, ZR, zpeer)
+    kept = over_y(0)
+    mail.take(zr, ZR)
+    whole = (kept + zr[...].astype(F32)).astype(BF)
     for f in range(2):
-        total = over_y(f)
-        zs[2 + f] = total.astype(BF)
-        mail.post(zs.at[2 + f], zr.at[f], ZR + f, zpeer, home)
-    for f in range(2):
-        mail.take(zr.at[f], ZR + f, away)
-
-    def spread():
-        for f in range(2):
-            whole = (over_y(f) + zr[f].astype(F32)).astype(BF)
-            back[f] = dot(loose, whole).astype(BF).reshape(back.shape[1:])
-
-    pl.when(home)(spread)
-    for f, e, off, to in feeds:
-        mail.post(back.at[f, e], ret.at[own_group], RET + own_group, to, (away | (c == f)) if off == 0 else away)
-    last = pltpu.make_async_copy(back.at[c, own_group], ret.at[own_group], local.at[NX + 2])
-    pl.when(home)(last.start)
+        back[f] = dot(loose, whole[:, f * feats:(f + 1) * feats]).astype(BF).reshape(back.shape[1:])
+    for f, j, to in feeds:
+        mail.post(back.at[f, j], ret.at[own_group], RET + own_group, to, is_me(f, j))
+    last = pltpu.make_async_copy(back.at[c, turn_j], ret.at[own_group], local.at[NX + 2])
+    pl.when(mine)(last.start)
 
     enter()
     for piece in range(pieces):
@@ -427,9 +420,9 @@
     upper = blend.astype(BF)
     lower = (blend - upper.astype(F32)).astype(BF)
 
-    pl.when(home)(last.wait)
-    for e, off in zip(groups, order):
-        mail.take(ret.at[e], RET + e, home if off == 0 else None)
+    pl.when(mine)(last.wait)
+    for near_one, e, to in targets:
+        mail.take(ret.at[e], RET + e, mine if near_one else None)
     rows_in = ret[...].reshape(experts * PAD, -1)
     turn = (((0,), (0,)), ((), ()))
     out[...] = (lax.dot_general(upper, rows_in, turn, preferred_element_type=F32)
@@ -442,7 +435,7 @@
     tokens, feats = hidden.shape
     channels, states = x_in.shape[1], a_log.shape[0]
     tiles, quarter = channels // 128, states // NY
-    rows, ff = CAP * 8, w_gate.shape[1] // NX
+    rows, ff = CAP * SHARE, w_gate.shape[1] // NX
     vm = pl.BlockSpec(memory_space=pltpu.VMEM)
     hbm = pl.BlockSpec(memory_space=pl.ANY)
     sm = pl.BlockSpec(memory_space=pltpu.SMEM)
@@ -459,20 +452,21 @@
             pltpu.VMEM((2, NX, feats, ff), BF),
             pltpu.VMEM((2, NX * ff, feats), BF),
             pltpu.VMEM((8, PAD, feats), BF),
-            pltpu.VMEM((2, 8, PAD, feats), BF),
-            pltpu.VMEM((4, 2, rows, feats), BF),
-            pltpu.VMEM((len(BATCHES), 5, rows, ff), BF),
-            pltpu.VMEM((len(BATCHES), 3, rows, ff), BF),
-            pltpu.VMEM((len(BATCHES), NX, rows, ff), BF),
-            pltpu.VMEM((4, 2, rows, feats), BF),
-            pltpu.VMEM((2, rows, feats), BF),
-            pltpu.VMEM((4, rows, feats), BF),
-            pltpu.VMEM((4, rows, feats), BF),
-            pltpu.VMEM((2, rows, feats), BF),
-            pltpu.VMEM((2, 8, PAD, feats), BF),
+            pltpu.VMEM((2, SHARE, PAD, feats), BF),
+            pltpu.VMEM((4, 2, rows, 2 * feats), BF),
+            pltpu.VMEM((len(BATCHES), 5, 2, rows, ff), BF),
+            pltpu.VMEM((len(BATCHES), 3, 2, rows, ff), BF),
+            pltpu.VMEM((len(BATCHES), NX, 2, rows, ff), BF),
+            pltpu.VMEM((4, 2, rows, 2 * feats), BF),
+            pltpu.VMEM((2, 2, rows, 2 * feats), BF),
+            pltpu.VMEM((2, 2, rows, feats), BF),
+            pltpu.VMEM((2, 2, rows, 2 * feats), BF),
+            pltpu.VMEM((rows, 2 * feats), BF),
+            pltpu.VMEM((2, SHARE, PAD, feats), BF),
             pltpu.VMEM((8, PAD, feats), BF),
             pltpu.VMEM((8, 128), F32),
             pltpu.VMEM((8, 8, 128), F32),
+            pltpu.VMEM((rows, 2 * feats), BF),
             pltpu.VMEM((16, channels), BF),
             pltpu.VMEM((8 + tokens, channels), F32),
             pltpu.VMEM((tokens, channels), F32),

time: 113 us -> 110 us (0.973)
  Pallas kernels: 109 us -> 106 us
    pallas_call x1, Pallas kernels: 109 us -> 106 us  [local(): pl.pallas_call(layer_kernel, out_shape=(jax.ShapeDtypeStruct((tokens, cha...]
where the time goes in v4:
time: 110 us
  Pallas kernels  106 us (96%)
  local copies, waits for them, and re-layouts  3.04 us (3%)
    pallas_call x1, Pallas kernels, local(): pl.pallas_call(layer_kernel, out_shape=(jax.ShapeDtypeStruct((tokens, cha...  106 us
    unnamed x2, local copies, waits for them, and re-layouts  3.04 us

profile of v4, /device:TPU:1, one launch (start us, length us, event | category | flops | bytes accessed | tf_op | source)
XLA Modules:
  0.0 109.7 jit_solution(18424218701652435649)
XLA Ops:
  0.6 106.1 %layer.1 = (bf16[64,1024]{1,0:T(8,128)(2,1)}, bf16[64,512]{1,0:T(8,128)(2,1)}) custom-call(bf16[64,1024]{1,0:T(8,128)(2,1)} %x_in.1, bf16[64,1024]{1,0:T(8,128)(2,1)} %z_gate.1, bf16[64,256]{1,0:T(8,128)(2,1)} %dt_low.1, bf16[256,1024]{1,0:T(8,128)(2,1)} %dt_weight.1, f32[1,1024]{1,0:T(1,128)} %bitcast.6, f32[16,1024]{1,0:T(8,128)} %a_log.1, ...), custom_call_target="tpu_custom_call" | custom-call | tf_op jit(solution)/shard_map/layer/pallas_call | solution.py:446
  106.7 1.6 %copy.19 = bf16[64,1024]{1,0:T(8,128)(2,1)} copy(bf16[64,1024]{1,0:T(8,128)(2,1)} %get-tuple-element.4) | data formatting | bytes 262144
  108.3 1.5 %copy.20 = bf16[64,512]{1,0:T(8,128)(2,1)} copy(bf16[64,512]{1,0:T(8,128)(2,1)} %get-tuple-element.5) | data formatting | bytes 131072

commit v5 on v4

--- a/solution.py
+++ b/solution.py
@@ -10,6 +10,7 @@
 CAP = 18
 PAD = 24
 NZ, NY, NX = 16, 4, 4
+DIRECT = 4
 MESH = pl.DeviceIdType.MESH
 BF, F32 = jnp.bfloat16, jnp.float32
 SHARE = 4
@@ -52,11 +53,12 @@
                 pl.when(jnp.logical_not(unless))(copy.wait_send)
 
 
-def layer_kernel(x_in, z_gate, dt_low, dt_weight, dt_bias, a_log, conv_weight, conv_bias, d_skip, b_and_c,
-                 hid, router_t, ids_t, wg_in, wd_in, mixed, out,
-                 wg, wd, pack, in1, rt, sbuf, rbuf, act, prod, ys, yc, zs, zr, back, ret, lgs, lgr, zb,
-                 tail, padded, active, delta, drive, rates, factor, state, rowend, rowall, zall, entry, reads,
-                 send, recv, local):
+def layer_kernel(x_in_hbm, z_gate_hbm, dt_low_hbm, dt_weight_hbm, dt_bias_hbm, a_log_hbm, conv_weight_hbm, conv_bias_hbm,
+                 d_skip_hbm, b_and_c, hid_hbm, router_t_hbm, ids_t, wg_in, wd_in, mixed, out, wg, wd, pack,
+                 in1, rt, sbuf, rbuf, act, prod, ys, yc, zs, zr, back, ret, lgs, lgr, zb, prior, tail, padded,
+                 active, delta, drive, rates, factor, state, rowend, rowall, zall, entry, reads, send, recv,
+                 local, intake, x_in, z_gate, dt_low, dt_weight, dt_bias, a_log, conv_weight, conv_bias,
+                 d_skip, hid, router_t):
     seq, exp = lax.axis_index("seq"), lax.axis_index("exp")
     z, y, x, c = seq // NY, lax.rem(seq, NY), exp // 2, lax.rem(exp, 2)
     half = lax.rem(z, 2)
@@ -72,6 +74,7 @@
     ypeer = {d: at(z, near[d], x, c) for d in (1, -1)}
     xpeer = {d: at(z, y, xs[d], c) for d in (1, -1)}
     zpeer = at(zpair, y, x, c)
+    xfar = at(z, y, xs[2], c)
     experts = 8
 
     barrier = pltpu.get_barrier_semaphore()
@@ -114,6 +117,19 @@
 
     lax.fori_loop(0, z, greet_earlier, 0)
 
+    staged = {}
+    for n, (source, target) in enumerate((
+            (hid_hbm, hid), (router_t_hbm, router_t), (x_in_hbm, x_in),
+            (z_gate_hbm, z_gate),
+            (dt_low_hbm, dt_low),
+            (dt_weight_hbm, dt_weight),
+            (dt_bias_hbm, dt_bias),
+            (a_log_hbm, a_log),
+            (conv_weight_hbm, conv_weight),
+            (conv_bias_hbm, conv_bias),
+            (d_skip_hbm, d_skip))):
+        staged[n] = pltpu.make_async_copy(source, target, intake.at[n])
+        staged[n].start()
     loads = []
     for q in range(NX):
         loads.append(pltpu.make_async_copy(wg_in.at[:, pl.ds(q * ff, ff)], wg.at[c, q], local.at[q]))
@@ -121,6 +137,8 @@
     for copy in loads:
         copy.start()
 
+    for n in (0, 1):
+        staged[n].wait()
     ids = ids_t[...]
     tokens = ids.shape[1]
     e_iota = lax.broadcasted_iota(jnp.int32, (experts, tokens), 0)
@@ -147,6 +165,8 @@
     group_e = sum((r_e >= CAP * m).astype(jnp.int32) for m in range(1, SHARE))
     loose = jnp.where(q_e == r_e + (PAD - CAP) * group_e, 1.0, 0.0).astype(BF)
 
+    for n in range(2, len(staged)):
+        staged[n].wait()
     channels = x_in.shape[1]
     tiles = channels // 128
 
@@ -217,24 +237,27 @@
         mail.post(rt.at[0, w], rt.at[1, w], RT + 2 + w, ypeer[-1])
         mail.post(rt.at[0, w], rt.at[0, w], RT + w, zpeer)
     quarter = states // NY
-    for to_y in (near[1], near[-1], yfar):
-        mail.take(rowend.at[to_y], ROW + to_y)
-    ahead_sum, row_sum = blank, blank
-    for other_y in range(NY):
-        ahead_sum = jnp.where(y == other_y, row_sum, ahead_sum)
-        row_sum = row_sum + rowend[other_y, states]
-    for n in range(states):
-        total, mine_before = blank, blank
+
+    def along_y():
+        for to_y in (near[1], near[-1], yfar):
+            mail.take(rowend.at[to_y], ROW + to_y)
+        ahead_sum, row_sum = blank, blank
         for other_y in range(NY):
-            mine_before = jnp.where(y == other_y, total, mine_before)
-            total = jnp.exp(rates[n] * rowend[other_y, states]) * total + rowend[other_y, n]
-        state[n] = mine_before
-        rowall[n // quarter, n % quarter] = total
-    for i in range(NY):
-        rowall[i, quarter] = row_sum
-    for later in range(1, NZ):
-        gone = z + later >= NZ
-        mail.post(rowall.at[y], zall.at[z], ZALL + z, at(jnp.where(gone, z, z + later), y, x, c), gone)
+            ahead_sum = jnp.where(y == other_y, row_sum, ahead_sum)
+            row_sum = row_sum + rowend[other_y, states]
+        for n in range(states):
+            total, mine_before = blank, blank
+            for other_y in range(NY):
+                mine_before = jnp.where(y == other_y, total, mine_before)
+                total = jnp.exp(rates[n] * rowend[other_y, states]) * total + rowend[other_y, n]
+            state[n] = mine_before
+            rowall[n // quarter, n % quarter] = total
+        for i in range(NY):
+            rowall[i, quarter] = row_sum
+        for later in range(1, NZ):
+            gone = z + later >= NZ
+            mail.post(rowall.at[y], zall.at[z], ZALL + z, at(jnp.where(gone, z, z + later), y, x, c), gone)
+        prior[...] = ahead_sum
 
     def along_z():
         def fold(other_z, carry):
@@ -253,7 +276,7 @@
         for to_y in (near[1], near[-1], yfar):
             mail.take(entry.at[to_y], ENTRY + to_y)
         for n in range(states):
-            state[n] = state[n] + jnp.exp(rates[n] * ahead_sum) * entry[n // quarter, n % quarter]
+            state[n] = state[n] + jnp.exp(rates[n] * prior[...]) * entry[n // quarter, n % quarter]
 
     pieces = 4
 
@@ -320,7 +343,15 @@
         d, r = way[b], span(b)
         for i in blocks(b):
             sbuf[b, 0, i] = part(b, i, xs[2]).astype(BF)
-        mail.post(sbuf.at[b, 0, r], rbuf.at[b, 0, r], RS + 3 * b, xpeer[d])
+        mail.post(sbuf.at[b, 0, r], rbuf.at[b, 0, r], RS + 3 * b, xfar if b == DIRECT else xpeer[d])
+        if b == DIRECT:
+            for slot, way_to in ((1, -d), (2, d)):
+                for i in blocks(b):
+                    sbuf[b, slot, i] = part(b, i, xs[way_to]).astype(BF)
+                mail.post(sbuf.at[b, slot, r], rbuf.at[b, slot, r], RS + 3 * b + slot, xpeer[way_to])
+            for i in blocks(b):
+                sbuf[b, 3, i] = part(b, i, x).astype(BF)
+            return
         for i in blocks(b):
             sbuf[b, 1, i] = part(b, i, xs[-d]).astype(BF)
         mail.post(sbuf.at[b, 1, r], rbuf.at[b, 1, r], RS + 3 * b + 1, xpeer[-d])
@@ -337,13 +368,17 @@
 
     def third(b):
         r = span(b)
+        if b == DIRECT:
+            mail.take(rbuf.at[b, 0, r], RS + 3 * b)
         mail.take(rbuf.at[b, 1, r], RS + 3 * b + 1)
         mail.take(rbuf.at[b, 2, r], RS + 3 * b + 2)
         for i in blocks(b):
             total = sbuf[b, 3, i].astype(F32) + rbuf[b, 1, i].astype(F32) + rbuf[b, 2, i].astype(F32)
+            if b == DIRECT:
+                total += rbuf[b, 0, i].astype(F32)
             act[b, x, i] = jax.nn.silu(total).astype(BF)
-        for d in (1, -1):
-            mail.post(act.at[b, x, r], act.at[b, x, r], ACT + 4 * b + x, xpeer[d])
+        for to in (xpeer[1], xpeer[-1]) + ((xfar,) if b == DIRECT else ()):
+            mail.post(act.at[b, x, r], act.at[b, x, r], ACT + 4 * b + x, to)
 
     def fourth(b):
         d, r = way[b], span(b)
@@ -353,6 +388,8 @@
     def down(b):
         d, r = way[b], span(b)
         mail.take(act.at[b, xs[d], r], ACT + 4 * b + xs[d])
+        if b == DIRECT:
+            mail.take(act.at[b, xs[-d], r], ACT + 4 * b + xs[-d])
         mail.take(act.at[b, xs[2], r], ACT + 4 * b + xs[2])
         for i in blocks(b):
             k, w = BATCHES[b][i]
@@ -378,9 +415,9 @@
     steps = [
         (first, 0), (gathered, 1, 0), (gathered, 2, 0), (gathered, 0, 1), (first, 1), (second, 0), (gathered, 3, 0),
         (third, 0), (second, 1), (gathered, 1, 1), (gathered, 2, 1), (fourth, 0), (gathered, 3, 1), (first, 2),
-        (third, 1), (first, 3), (second, 2), (fourth, 1), (take_down,), (down, 0), (first, 4), (second, 3), (third, 2),
-        (down, 1), (along_z,), (second, 4), (fourth, 2), (third, 3), (down, 2), (far, 0), (far, 1), (third, 4),
-        (fourth, 3), (combine, 0), (down, 3), (combine, 1), (fourth, 4), (down, 4)]
+        (third, 1), (first, 3), (along_y,), (second, 2), (fourth, 1), (take_down,), (down, 0), (first, 4), (second, 3), (third, 2),
+        (down, 1), (fourth, 2), (third, 3), (down, 2), (far, 0), (far, 1), (along_z,), (third, 4),
+        (fourth, 3), (combine, 0), (down, 3), (combine, 1), (down, 4)]
     for step_of, *which in steps:
         step_of(*which)
 
@@ -390,15 +427,18 @@
             mail.take(ys.at[w, f], YS + 2 * w + f)
         return prod[0, w].astype(F32) + ys[w, 0].astype(F32) + ys[w, 1].astype(F32)
 
-    zb[...] = over_y(1).astype(BF)
-    mail.post(zb, zr, ZR, zpeer)
+    passed, kept = over_y(1), None
+    for f in range(2):
+        zb[f] = passed[:, f * feats:(f + 1) * feats].astype(BF)
+        mail.post(zb.at[f], zr.at[f], ZR + 47 * f, zpeer)
     kept = over_y(0)
-    mail.take(zr, ZR)
-    whole = (kept + zr[...].astype(F32)).astype(BF)
     for f in range(2):
-        back[f] = dot(loose, whole[:, f * feats:(f + 1) * feats]).astype(BF).reshape(back.shape[1:])
-    for f, j, to in feeds:
-        mail.post(back.at[f, j], ret.at[own_group], RET + own_group, to, is_me(f, j))
+        mail.take(zr.at[f], ZR + 47 * f)
+        whole = (kept[:, f * feats:(f + 1) * feats] + zr[f].astype(F32)).astype(BF)
+        back[f] = dot(loose, whole).astype(BF).reshape(back.shape[1:])
+        for g, j, to in feeds:
+            if g == f:
+                mail.post(back.at[f, j], ret.at[own_group], RET + own_group, to, is_me(f, j))
     last = pltpu.make_async_copy(back.at[c, turn_j], ret.at[own_group], local.at[NX + 2])
     pl.when(mine)(last.start)
 
@@ -446,7 +486,7 @@
     return pl.pallas_call(
         layer_kernel,
         out_shape=(jax.ShapeDtypeStruct((tokens, channels), BF), jax.ShapeDtypeStruct((tokens, feats), BF)),
-        in_specs=[vm] * 9 + [sm] + [vm] * 3 + [hbm] * 2,
+        in_specs=[hbm] * 9 + [sm] + [hbm] * 2 + [vm] + [hbm] * 2,
         out_specs=(vm, vm),
         scratch_shapes=[
             pltpu.VMEM((2, NX, feats, ff), BF),
@@ -461,12 +501,13 @@
             pltpu.VMEM((2, 2, rows, 2 * feats), BF),
             pltpu.VMEM((2, 2, rows, feats), BF),
             pltpu.VMEM((2, 2, rows, 2 * feats), BF),
-            pltpu.VMEM((rows, 2 * feats), BF),
+            pltpu.VMEM((2, rows, feats), BF),
             pltpu.VMEM((2, SHARE, PAD, feats), BF),
             pltpu.VMEM((8, PAD, feats), BF),
             pltpu.VMEM((8, 128), F32),
             pltpu.VMEM((8, 8, 128), F32),
-            pltpu.VMEM((rows, 2 * feats), BF),
+            pltpu.VMEM((2, rows, feats), BF),
+            pltpu.VMEM((tiles, 128), F32),
             pltpu.VMEM((16, channels), BF),
             pltpu.VMEM((8 + tokens, channels), F32),
             pltpu.VMEM((tokens, channels), F32),
@@ -483,6 +524,18 @@
             pltpu.SemaphoreType.DMA((128,)),
             pltpu.SemaphoreType.DMA((128,)),
             pltpu.SemaphoreType.DMA((8,)),
+            pltpu.SemaphoreType.DMA((16,)),
+            pltpu.VMEM((tokens, channels), BF),
+            pltpu.VMEM((tokens, channels), BF),
+            pltpu.VMEM(dt_low.shape, BF),
+            pltpu.VMEM(dt_weight.shape, BF),
+            pltpu.VMEM((1, channels), F32),
+            pltpu.VMEM(a_log.shape, F32),
+            pltpu.VMEM(conv_weight.shape, F32),
+            pltpu.VMEM((1, channels), F32),
+            pltpu.VMEM((1, channels), F32),
+            pltpu.VMEM(hidden.shape, BF),
+            pltpu.VMEM(router.shape[::-1], BF),
         ],
         compiler_params=pltpu.CompilerParams(collective_id=0, has_side_effects=True,
                                              vmem_limit_bytes=60 * 1024 * 1024),

time: 110 us -> 103 us (0.936)
  Pallas kernels: 106 us -> 98.4 us
    pallas_call x1, Pallas kernels: 106 us -> 98.4 us  [local(): pl.pallas_call(layer_kernel, out_shape=(jax.ShapeDtypeStruct((tokens, cha...]
where the time goes in v5:
time: 103 us; the launch traced here: 102 us
  Pallas kernels  98.4 us (96%)
  local copies, waits for them, and re-layouts  3.04 us (3%)
    pallas_call x1, Pallas kernels, local(): pl.pallas_call(layer_kernel, out_shape=(jax.ShapeDtypeStruct((tokens, cha...  98.4 us
    unnamed x2, local copies, waits for them, and re-layouts  3.04 us

profile of v5, /device:TPU:1, one launch (start us, length us, event | category | flops | bytes accessed | tf_op | source)
XLA Modules:
  0.0 102.1 jit_solution(7832660252302105209)
XLA Ops:
  0.6 98.4 %layer.1 = (bf16[64,1024]{1,0:T(8,128)(2,1)}, bf16[64,512]{1,0:T(8,128)(2,1)}) custom-call(bf16[64,1024]{1,0:T(8,128)(2,1)} %x_in_hbm.1, bf16[64,1024]{1,0:T(8,128)(2,1)} %z_gate_hbm.1, bf16[64,256]{1,0:T(8,128)(2,1)} %dt_low_hbm.1, bf16[256,1024]{1,0:T(8,128)(2,1)} %dt_weight_hbm.1, f32[1,1024]{1,0:T(1,128)} %bitcast.6, f32[16,1024]{1,0:T(8,128)} %a_log_hbm.1, ...), custom_call_target="tpu_custom_call" | custom-call | tf_op jit(solution)/shard_map/layer/pallas_call | solution.py:486
  99.1 1.6 %copy.19 = bf16[64,1024]{1,0:T(8,128)(2,1)} copy(bf16[64,1024]{1,0:T(8,128)(2,1)} %get-tuple-element.4) | data formatting | bytes 262144
  100.7 1.5 %copy.20 = bf16[64,512]{1,0:T(8,128)(2,1)} copy(bf16[64,512]{1,0:T(8,128)(2,1)} %get-tuple-element.5) | data formatting | bytes 131072

commit v6 on v5

--- a/solution.py
+++ b/solution.py
@@ -416,7 +416,7 @@
         (first, 0), (gathered, 1, 0), (gathered, 2, 0), (gathered, 0, 1), (first, 1), (second, 0), (gathered, 3, 0),
         (third, 0), (second, 1), (gathered, 1, 1), (gathered, 2, 1), (fourth, 0), (gathered, 3, 1), (first, 2),
         (third, 1), (first, 3), (along_y,), (second, 2), (fourth, 1), (take_down,), (down, 0), (first, 4), (second, 3), (third, 2),
-        (down, 1), (fourth, 2), (third, 3), (down, 2), (far, 0), (far, 1), (along_z,), (third, 4),
+        (down, 1), (fourth, 2), (third, 3), (down, 2), (far, 0), (far, 1), (third, 4),
         (fourth, 3), (combine, 0), (down, 3), (combine, 1), (down, 4)]
     for step_of, *which in steps:
         step_of(*which)
@@ -431,6 +431,7 @@
     for f in range(2):
         zb[f] = passed[:, f * feats:(f + 1) * feats].astype(BF)
         mail.post(zb.at[f], zr.at[f], ZR + 47 * f, zpeer)
+    along_z()
     kept = over_y(0)
     for f in range(2):
         mail.take(zr.at[f], ZR + 47 * f)
@@ -470,6 +471,16 @@
     mail.finish()
 
 
+def deliver(a, b, a_out, b_out, a_held, b_held, sems):
+    ways = ((a, a_held, a_out), (b, b_held, b_out))
+    for leg in range(2):
+        copies = [pltpu.make_async_copy(way[leg], way[leg + 1], sems.at[n]) for n, way in enumerate(ways)]
+        for copy in copies:
+            copy.start()
+        for copy in copies:
+            copy.wait()
+
+
 def local(x_in, z_gate, dt_low, dt_weight, dt_bias, a_log, conv_weight, conv_bias, d_skip, b_and_c,
           hidden, router, expert_ids, w_gate, w_down):
     tokens, feats = hidden.shape
@@ -480,12 +491,14 @@
     hbm = pl.BlockSpec(memory_space=pl.ANY)
     sm = pl.BlockSpec(memory_space=pltpu.SMEM)
 
+    results_shape = (jax.ShapeDtypeStruct((tokens, channels), BF), jax.ShapeDtypeStruct((tokens, feats), BF))
+
     def row(a):
         return a.reshape(1, channels)
 
-    return pl.pallas_call(
+    results = pl.pallas_call(
         layer_kernel,
-        out_shape=(jax.ShapeDtypeStruct((tokens, channels), BF), jax.ShapeDtypeStruct((tokens, feats), BF)),
+        out_shape=results_shape,
         in_specs=[hbm] * 9 + [sm] + [hbm] * 2 + [vm] + [hbm] * 2,
         out_specs=(vm, vm),
         scratch_shapes=[
@@ -542,6 +555,9 @@
         name="layer",
     )(x_in, z_gate, dt_low, dt_weight, row(dt_bias), a_log, conv_weight, row(conv_bias), row(d_skip), b_and_c,
       hidden, router.T, expert_ids.T, w_gate, w_down)
+    return pl.pallas_call(deliver, out_shape=results_shape, in_specs=[hbm] * 2, out_specs=(hbm, hbm),
+                          scratch_shapes=[pltpu.VMEM((tokens, channels), BF), pltpu.VMEM((tokens, feats), BF),
+                                          pltpu.SemaphoreType.DMA((2,))], name="deliver")(*results)
 
 
 def solution(mesh):

time: 103 us -> 101 us (0.981)
  local copies, waits for them, and re-layouts: 3.04 us -> 0 us
  Pallas kernels: 98.4 us -> 99.9 us
    unnamed x2 -> x0, local copies, waits for them, and re-layouts: 3.04 us -> none
    pallas_call x1 -> x2, Pallas kernels: 98.4 us -> 99.9 us  [the longest x1 98.3 us: local(): pl.pallas_call(layer_kernel, out_shape=results_shape, in_specs=[hbm] * 9...]
where the time goes in v6:
time: 101 us
  Pallas kernels  99.9 us (99%)
    pallas_call x1, Pallas kernels, local(): pl.pallas_call(layer_kernel, out_shape=results_shape, in_specs=[hbm] * 9...  98.3 us

profile of v6, /device:TPU:1, one launch (start us, length us, event | category | flops | bytes accessed | tf_op | source)
XLA Modules:
  0.0 100.6 jit_solution(18018860221990994790)
XLA Ops:
  0.6 98.3 %layer.1 = (bf16[64,1024]{1,0:T(8,128)(2,1)}, bf16[64,512]{1,0:T(8,128)(2,1)}) custom-call(bf16[64,1024]{1,0:T(8,128)(2,1)} %x_in_hbm.1, bf16[64,1024]{1,0:T(8,128)(2,1)} %z_gate_hbm.1, bf16[64,256]{1,0:T(8,128)(2,1)} %dt_low_hbm.1, bf16[256,1024]{1,0:T(8,128)(2,1)} %dt_weight_hbm.1, f32[1,1024]{1,0:T(1,128)} %bitcast.6, f32[16,1024]{1,0:T(8,128)} %a_log_hbm.1, ...), custom_call_target="tpu_custom_call" | custom-call | tf_op jit(solution)/shard_map/layer/pallas_call | solution.py:499
  99.0 1.6 %deliver.1 = (bf16[64,1024]{1,0:T(8,128)(2,1)}, bf16[64,512]{1,0:T(8,128)(2,1)}) custom-call(bf16[64,1024]{1,0:T(8,128)(2,1)} %get-tuple-element.4.a, bf16[64,512]{1,0:T(8,128)(2,1)} %get-tuple-element.5.b), custom_call_target="tpu_custom_call" | custom-call | tf_op jit(solution)/shard_map/deliver/pallas_call | solution.py:558
